TPU v7x, 32 devices: a whole 2x2x4 slice. The times are simulated.
32 devices in a mesh: col: 8 (over z, x), tile: 4 (over y, core).
Axes of the slice: x: 2, y: 2, z: 4, core: 2. Of those that a mesh axis runs over, the one named last changes fastest.
Arguments:
- initial_image: float32 [16384, 1024], P('tile', 'col'), may hold values from -6 to 6
- panels: float32 [8, 256, 16384], P('col', None, 'tile'), may hold values from -0.046875 to 0.046875
- sinogram: float32 [8, 256, 1024], P(None, 'tile', 'col'), may hold values from -6 to 6
- subset_order: int32 [3], replicated, may hold values from 0 to 7
- step_sizes: float32 [3], replicated, may hold values from 0.5 to 1
Outputs:
- final_image: float32 [16384, 1024], P('tile', 'col')
- final_duals: float32 [8, 256, 1024], P(None, 'tile', 'col')
Inputs may be any that keep to these rules, and one draw needn't show every extreme that they name: `subset_order`: repeats may occur.
All inputs are finite; a program needn't handle non-finite values.
Results may differ from a plain program's by a relative error of at most 0.00013.
Values sent between devices are 32-bit elements; how exact they have to be, the bound alone decides.
No kernel may reach another device: no remote copies, remote signals or barrier semaphores. Data moves between devices by JAX's collectives and lax.ppermute only.
A program may use at most 128 MiB of HBM per device.

v0:
```python
import jax
import jax.numpy as jnp
from jax import lax
from jax.sharding import PartitionSpec as P

WIDTH = 512
ITERS = 3


penalty = 0.2
smoothing = 1.0


def shifted(value, axis, by):
    count = lax.axis_size(axis)
    pairs = [(i, i + by) for i in range(count) if 0 <= i + by < count]
    return lax.ppermute(value, axis, pairs)


def broadcast(value, axis, root):
    mine = lax.axis_index(axis) == root
    return lax.psum(jnp.where(mine, value, jnp.zeros_like(value)), axis)


def divergence(estimate, rows_local, tile_index, total_rows):
    channels = estimate.shape[1]
    image_field = estimate.reshape(rows_local, WIDTH, channels)
    row_below = shifted(image_field[0:1], "tile", -1)
    extended = jnp.concatenate([image_field, row_below], axis=0)
    downward = extended[1:] - extended[:-1]
    global_row = tile_index * rows_local + lax.broadcasted_iota(jnp.int32, (rows_local, 1, 1), 0)
    downward = jnp.where(global_row < total_rows - 1, downward, jnp.zeros_like(downward))
    column_zero = jnp.zeros((rows_local, 1, channels), estimate.dtype)
    across = jnp.concatenate([image_field[:, 1:] - image_field[:, :-1], column_zero], axis=1)
    magnitude = jnp.sqrt(across * across + downward * downward + smoothing * smoothing)
    flux_across = across / magnitude
    flux_down = downward / magnitude
    flux_above = shifted(flux_down[rows_local - 1 :], "tile", 1)
    shifted_across = jnp.concatenate([column_zero, flux_across[:, :-1]], axis=1)
    shifted_down = jnp.concatenate([flux_above, flux_down[:-1]], axis=0)
    divergence_field = flux_across - shifted_across + flux_down - shifted_down
    return divergence_field.reshape(estimate.shape)


def per_device(initial_image, panels, sinogram, subset_order, step_sizes):
    dual_step = step_sizes[0]
    primal_step = step_sizes[1]
    extrapolate = step_sizes[2]
    tile_count = lax.axis_size("tile")
    tile_index = lax.axis_index("tile")
    rows_local = initial_image.shape[0] // WIDTH
    total_rows = rows_local * tile_count
    stored = panels.shape[0]
    rays_local = panels.shape[1] // tile_count
    subset_count = sinogram.shape[0]

    def primal(estimate, extrapolated):
        field_div = divergence(estimate, rows_local, tile_index, total_rows)
        return estimate - primal_step * extrapolated + primal_step * penalty * field_div

    estimate = initial_image
    dual_state = jnp.zeros(sinogram.shape, jnp.float32)
    accumulated = jnp.zeros(initial_image.shape, jnp.float32)
    extrapolated = jnp.zeros(initial_image.shape, jnp.float32)
    for iteration in range(ITERS):
        estimate = primal(estimate, extrapolated)
        subset = subset_order[iteration]
        owner_index = subset // stored
        own_panel = lax.dynamic_index_in_dim(panels, subset % stored, 0, keepdims=False)
        operator_panel = broadcast(own_panel, "col", owner_index)
        current = lax.dynamic_index_in_dim(dual_state, subset, 0, keepdims=False)
        measured = lax.dynamic_index_in_dim(sinogram, subset, 0, keepdims=False)

        def partial_rows(first_row, row_count, operator_panel=operator_panel, estimate=estimate):
            return jnp.dot(
                operator_panel,
                estimate,
                precision=lax.Precision.HIGHEST,
                preferred_element_type=jnp.float32,
            )

        forward = lax.psum_scatter(
            partial_rows(jnp.int32(0), rays_local * lax.axis_size("tile")),
            "tile",
            scatter_dimension=0,
            tiled=True,
        )
        updated = (current + dual_step * forward - dual_step * measured) / (1.0 + dual_step)
        change = updated - current

        def add_back(running, received, first_row, operator_panel=operator_panel):
            return lax.dot_general(
                operator_panel,
                received,
                (((0,), (0,)), ((), ())),
                precision=lax.Precision.HIGHEST,
                preferred_element_type=jnp.float32,
            )

        adjoint = add_back(
            jnp.zeros(estimate.shape, jnp.float32),
            lax.all_gather(change, "tile", axis=0, tiled=True),
            jnp.int32(0),
        )
        dual_state = lax.dynamic_update_index_in_dim(dual_state, updated, subset, 0)
        accumulated = accumulated + adjoint
        extrapolated = accumulated + extrapolate * subset_count * adjoint
    final_image = primal(estimate, extrapolated)
    return (final_image, dual_state)


def solution(mesh):
    in_specs = (P("tile", "col"), P("col", None, "tile"), P(None, "tile", "col"), P(), P())
    out_specs = (P("tile", "col"), P(None, "tile", "col"))
    return jax.shard_map(
        per_device, mesh=mesh, in_specs=in_specs, out_specs=out_specs, check_vma=False
    )
```

profile of v0, /device:TPU:0, one launch (start us, length us, event | category | flops | bytes accessed | tf_op | source)
XLA Modules:
  0.0 561.9 jit_solution(9093737235696430673)
XLA Ops:
  7.2 0.0 all-reduce.11.cloned.1.call-start
  7.2 1.4 fusion.30
  10.5 7.2 %select_bitcast_fusion = (f32[256,4096]{1,0:T(8,128)}, f32[256,4096]{1,0:T(8,128)}, f32[256,4096]{1,0:T(8,128)}) fusion(f32[1,256,4096]{2,1,0:T(8,128)} %param.6, pred[]{:T(512)S(6)} %eq.15, pred[]{:T(512)S(6)} %eq.13, pred[]{:T(512)S(6)} %eq.14), kind=kLoop, calls=%fused_computation | loop fusion | flops 3145728 | bytes 16777220 | tf_op jit(solution)/shard_map/jit(_where)/select_n | solution.py:22
  17.7 0.0 all-reduce.11.cloned.1.call-update
  17.7 0.0 reduce-scatter.4.cloned.1.call-start
  17.7 1.5 copy-done.4
  19.3 1.3 collective-permute-start
  20.6 0.2 slice_subtract_fusion.3
  20.8 1.9 collective-permute-done
  22.7 2.5 fusion.22
  25.2 1.4 copy-done.6
  26.6 8.1 %collective-permute-start.1 = (f32[1,512,128]{2,1,0:T(8,128)S(1)}, f32[1,512,128]{2,1,0:T(8,128)S(1)}, u32[]{:S(2)}, u32[]{:S(2)}) collective-permute-start(f32[1,512,128]{2,1,0:T(8,128)S(1)} %slice.155), channel_id=1, source_target_pairs={{0,1},{1,2},{2,3},{4,5},{5,6},{6,7},{8,9},{9,10},{10,11},{12,13},{... | collective-permute-start | bytes 786440 | tf_op jit(solution)/shard_map/ppermute | solution.py:17
  38.5 0.7 fusion.29
  43.6 1.6 slice.156
  45.2 2.9 fusion.11
  48.2 0.2 bitcast_add_fusion.2
  48.4 1.3 collective-permute-start.2
  49.7 0.2 slice_subtract_fusion.2
  49.9 1.9 collective-permute-done.2
  51.9 2.5 fusion.20
  54.4 1.5 slice.162
  55.8 0.4 copy-done.8
  56.2 6.6 %collective-permute-start.3 = (f32[1,512,128]{2,1,0:T(8,128)S(1)}, f32[1,512,128]{2,1,0:T(8,128)S(1)}, u32[]{:S(2)}, u32[]{:S(2)}) collective-permute-start(f32[1,512,128]{2,1,0:T(8,128)S(1)} %slice.161), channel_id=1, source_target_pairs={{0,1},{1,2},{2,3},{4,5},{5,6},{6,7},{8,9},{9,10},{10,11},{12,13},{... | collective-permute-start | bytes 786440 | tf_op jit(solution)/shard_map/ppermute | solution.py:17
  62.9 352.5 %all-reduce.11.cloned.1.call-done = (f32[256,4096]{1,0:T(8,128)}, f32[256,4096]{1,0:T(8,128)}, f32[256,4096]{1,0:T(8,128)}) async-done(((f32[256,4096]{1,0:T(8,128)}, f32[256,4096]{1,0:T(8,128)}, f32[256,4096]{1,0:T(8,128)}), (f32[256,4096]{1,0:T(8,128)}, f32[256,4096]{1,0:T(8,128)}, f32[256,4096]{1,0:T(8,128)})) %all-reduce.11.cloned.1.call-update) | async-done | bytes 12582928 | tf_op jit(solution)/shard_map/psum | solution.py:22
  415.4 5.9 %fusion.31 = f32[256,128]{1,0:T(8,128)} fusion(f32[256,4096]{1,0:T(8,128)} %get-tuple-element.2, f32[4096,128]{1,0:T(8,128)S(1)} %bitcast_add_fusion.2), kind=kOutput, calls=%fused_computation.66 | convolution fusion | flops 1610612736 | bytes 6422528 | tf_op jit(solution)/shard_map/dot_general | solution.py:75
  421.3 0.0 reduce-scatter.6.cloned.1.call-start
  421.3 5.1 fusion.12
  426.5 13.7 %reduce-scatter.4.cloned.1.call-done = f32[64,128]{1,0:T(8,128)} async-done(((f32[256,128]{1,0:T(8,128)}), f32[64,128]{1,0:T(8,128)}) %reduce-scatter.4.cloned.1.call-update) | async-done | bytes 32784 | tf_op jit(solution)/shard_map/reduce_scatter | solution.py:82
  440.2 1.3 bitcast_dynamic-update-slice_fusion.2
  441.5 5.6 all_gather.9
  447.1 11.9 %fusion.2 = (f32[4096,128]{1,0:T(8,128)S(1)}, f32[4096,128]{1,0:T(8,128)}) fusion(f32[4096,128]{1,0:T(8,128)S(1)} %bitcast_add_fusion.2, f32[8,512,128]{2,1,0:T(8,128)} %fusion.12, f32[]{:T(128)} %bitcast.8, f32[]{:T(128)} %bitcast, f32[256,4096]{1,0:T(8,128)} %get-tuple-element.2, f32[256,128]{1,0:T(8,128)S(1)} %all_gather.9), kind=kOutput, calls=%fused_computation.6 | convolution fusion | flops 1613234176 | bytes 12713992 | tf_op jit(solution)/shard_map/dot_general | solution.py:92
  459.0 1.3 copy-done
  460.3 4.1 fusion.32
  464.5 0.0 reduce-scatter.8.cloned.1.call-start
  464.5 1.3 collective-permute-start.4
  465.8 2.6 slice_subtract_fusion.1
  468.4 0.3 copy-done.1
  468.7 2.5 fusion.18
  471.2 1.5 slice.168
  472.7 0.4 copy-done.9
  473.1 5.8 %collective-permute-start.5 = (f32[1,512,128]{2,1,0:T(8,128)S(1)}, f32[1,512,128]{2,1,0:T(8,128)S(1)}, u32[]{:S(2)}, u32[]{:S(2)}) collective-permute-start(f32[1,512,128]{2,1,0:T(8,128)S(1)} %slice.167), channel_id=1, source_target_pairs={{0,1},{1,2},{2,3},{4,5},{5,6},{6,7},{8,9},{9,10},{10,11},{12,13},{... | collective-permute-start | bytes 786440 | tf_op jit(solution)/shard_map/ppermute | solution.py:17
  478.9 5.4 reduce-scatter.6.cloned.1.call-done
  484.3 1.3 bitcast_subtract_fusion.3
  485.6 5.6 %all_gather.10 = f32[256,128]{1,0:T(8,128)S(1)} all-gather(f32[64,128]{1,0:T(8,128)S(1)} %get-tuple-element.9), channel_id=1, replica_groups=mesh['col'=8,'tile'=4] {'tile'}, dimensions={0}, use_global_device_ids=true | all-gather | bytes 163840 | tf_op jit(solution)/shard_map/all_gather | solution.py:102
  491.3 4.0 fusion.13
  495.2 0.6 copy-done.13
  495.8 0.7 copy-done.14
  496.5 9.3 %bitcast_add_fusion.1 = (f32[4096,128]{1,0:T(8,128)S(1)}, f32[4096,128]{1,0:T(8,128)}) fusion(f32[8,512,128]{2,1,0:T(8,128)S(1)} %fusion.13, f32[4096,128]{1,0:T(8,128)S(1)} %copy-done.1, f32[]{:T(128)} %bitcast.8, f32[]{:T(128)} %bitcast, f32[4096,128]{1,0:T(8,128)S(1)} %copy-done.14, f32[256,4096]{1,0:T(8,128)S(1)} %copy-done.13, ...), kind=kOutput, calls=%fused_computation.32 | convolution fusion | flops 1613758464 | bytes 14811144 | tf_op jit(solution)/shard_map/dot_general | solution.py:92
  505.8 1.4 copy-done.2
  507.2 4.1 fusion.33
  511.3 0.0 reduce-scatter.8.cloned.1.call-update
  511.3 1.3 collective-permute-start.6
  512.7 4.0 slice_subtract_fusion
  516.6 14.6 %reduce-scatter.8.cloned.1.call-done = f32[64,128]{1,0:T(8,128)} async-done(((f32[256,128]{1,0:T(8,128)}), f32[64,128]{1,0:T(8,128)}) %reduce-scatter.8.cloned.1.call-update) | async-done | bytes 32784 | tf_op jit(solution)/shard_map/reduce_scatter | solution.py:82
  531.2 1.3 bitcast_subtract_fusion.1
  532.6 5.7 %all_gather.11 = f32[256,128]{1,0:T(8,128)S(1)} all-gather(f32[64,128]{1,0:T(8,128)S(1)} %get-tuple-element.5), channel_id=1, replica_groups=mesh['col'=8,'tile'=4] {'tile'}, dimensions={0}, use_global_device_ids=true | all-gather | bytes 163840 | tf_op jit(solution)/shard_map/all_gather | solution.py:102
  538.2 2.9 fusion.16
  541.2 2.3 collective-permute-start.7
  543.5 7.1 %fusion.34 = f32[4096,128]{1,0:T(8,128)S(1)} fusion(f32[256,4096]{1,0:T(8,128)S(1)} %copy-done.11, f32[256,128]{1,0:T(8,128)S(1)} %all_gather.11), kind=kOutput, calls=%fused_computation.69 | convolution fusion | flops 1610612736 | bytes 6422528 | tf_op jit(solution)/shard_map/dot_general | solution.py:92
  550.5 0.1 slice.174
  550.7 0.5 fusion.14
  551.2 0.2 copy-done.16
  551.4 1.0 copy-done.15
  552.4 2.5 bitcast_add_fusion
  (45 shorter events, 0.3 us)
Async XLA Ops:
  7.2 408.2 %all-reduce.11.cloned.1.call-start = ((), (), s32[]{:S(2)}) async-start(), calls=%async_computation.6 | async-start | bytes 25165824 | tf_op jit(solution)/shard_map/psum | solution.py:22
  17.7 1.6 copy-start.4
  17.7 422.5 %reduce-scatter.4.cloned.1.call-start = ((), (), s32[]{:S(2)}) async-start(), calls=%async_computation.3 | async-start | bytes 163840 | tf_op jit(solution)/shard_map/reduce_scatter | solution.py:82
  19.3 3.4 collective-permute-start
  20.8 17.7 %copy-start.17 = (f32[3]{0:T(128)S(1)}, f32[3]{0:T(128)}, u32[]{:S(2)}) copy-start(f32[3]{0:T(128)} %param.9) | copy-start | bytes 40
  25.2 1.4 copy-start.6
  26.6 18.6 %copy-start.7 = (f32[8,512,128]{2,1,0:T(8,128)S(1)}, f32[8,512,128]{2,1,0:T(8,128)}, u32[]{:S(2)}) copy-start(f32[8,512,128]{2,1,0:T(8,128)} %copy-done.6) | copy-start | bytes 6291460
  26.6 18.6 %collective-permute-start.1 = (f32[1,512,128]{2,1,0:T(8,128)S(1)}, f32[1,512,128]{2,1,0:T(8,128)S(1)}, u32[]{:S(2)}, u32[]{:S(2)}) collective-permute-start(f32[1,512,128]{2,1,0:T(8,128)S(1)} %slice.155), channel_id=1, source_target_pairs={{0,1},{1,2},{2,3},{4,5},{5,6},{6,7},{8,9},{9,10},{10,11},{12,13},{... | collective-permute-start | bytes 786440 | tf_op jit(solution)/shard_map/ppermute | solution.py:17
  45.2 3.0 copy-start.5
  48.4 3.4 collective-permute-start.2
  54.3 1.9 copy-start.8
  56.2 365.1 %collective-permute-start.3 = (f32[1,512,128]{2,1,0:T(8,128)S(1)}, f32[1,512,128]{2,1,0:T(8,128)S(1)}, u32[]{:S(2)}, u32[]{:S(2)}) collective-permute-start(f32[1,512,128]{2,1,0:T(8,128)S(1)} %slice.161), channel_id=1, source_target_pairs={{0,1},{1,2},{2,3},{4,5},{5,6},{6,7},{8,9},{9,10},{10,11},{12,13},{... | collective-permute-start | bytes 786440 | tf_op jit(solution)/shard_map/ppermute | solution.py:17
  421.3 63.0 %reduce-scatter.6.cloned.1.call-start = ((), (), s32[]{:S(2)}) async-start(), calls=%async_computation.4 | async-start | bytes 163840 | tf_op jit(solution)/shard_map/reduce_scatter | solution.py:82
  447.1 13.2 %copy-start.12 = (f32[256,4096]{1,0:T(8,128)S(1)}, f32[256,4096]{1,0:T(8,128)}, u32[]{:S(2)}) copy-start(f32[256,4096]{1,0:T(8,128)} %get-tuple-element.3) | copy-start | bytes 12582916
  459.0 1.3 copy-start
  464.5 66.7 %reduce-scatter.8.cloned.1.call-start = ((), (), s32[]{:S(2)}) async-start(), calls=%async_computation.5 | async-start | bytes 163840 | tf_op jit(solution)/shard_map/reduce_scatter | solution.py:82
  464.5 3.9 collective-permute-start.4
  465.8 2.9 copy-start.1
  471.2 1.9 copy-start.9
  473.1 18.2 %collective-permute-start.5 = (f32[1,512,128]{2,1,0:T(8,128)S(1)}, f32[1,512,128]{2,1,0:T(8,128)S(1)}, u32[]{:S(2)}, u32[]{:S(2)}) collective-permute-start(f32[1,512,128]{2,1,0:T(8,128)S(1)} %slice.167), channel_id=1, source_target_pairs={{0,1},{1,2},{2,3},{4,5},{5,6},{6,7},{8,9},{9,10},{10,11},{12,13},{... | collective-permute-start | bytes 786440 | tf_op jit(solution)/shard_map/ppermute | solution.py:17
  491.2 4.6 copy-start.13
  491.3 5.3 copy-start.14
  496.5 10.7 %copy-start.10 = (f32[256,4096]{1,0:T(8,128)S(1)}, f32[256,4096]{1,0:T(8,128)}, u32[]{:S(2)}) copy-start(f32[256,4096]{1,0:T(8,128)} %get-tuple-element.4) | copy-start | bytes 12582916
  505.8 1.4 copy-start.2
  511.3 26.9 %collective-permute-start.6 = (f32[1,512,128]{2,1,0:T(8,128)S(1)}, f32[1,512,128]{2,1,0:T(8,128)S(1)}, u32[]{:S(2)}, u32[]{:S(2)}) collective-permute-start(f32[1,512,128]{2,1,0:T(8,128)S(1)} %slice_bitcast_fusion), channel_id=1, source_target_pairs={{1,0},{2,1},{3,2},{5,4},{6,5},{7,6},{9,8},{10,9},{11,10},{13,12},{... | collective-permute-start | bytes 786440 | tf_op jit(solution)/shard_map/ppermute | solution.py:17
  512.6 25.6 %copy-start.3 = (f32[4096,128]{1,0:T(8,128)S(1)}, f32[4096,128]{1,0:T(8,128)}, u32[]{:S(2)}) copy-start(f32[4096,128]{1,0:T(8,128)} %copy-done.2) | copy-start | bytes 6291460
  538.2 5.2 copy-start.11
  541.2 9.5 %collective-permute-start.7 = (f32[1,512,128]{2,1,0:T(8,128)S(1)}, f32[1,512,128]{2,1,0:T(8,128)S(1)}, u32[]{:S(2)}, u32[]{:S(2)}) collective-permute-start(f32[1,512,128]{2,1,0:T(8,128)S(1)} %slice.173), channel_id=1, source_target_pairs={{0,1},{1,2},{2,3},{4,5},{5,6},{6,7},{8,9},{9,10},{10,11},{12,13},{... | collective-permute-start | bytes 786440 | tf_op jit(solution)/shard_map/ppermute | solution.py:17
  550.7 0.7 copy-start.16
  550.7 1.7 copy-start.15
Sparse Core Ops, SparseCore 0:
  17.8 397.5 all-reduce.10
  421.4 18.7 reduce-scatter.3
  464.6 19.6 reduce-scatter.5
  511.5 19.6 reduce-scatter.7
where the time goes:
time: 569 us; the launch traced here: 562 us
  waiting for transfers between devices  390 us (69%)
  other arithmetic  43.8 us (8%)
  matrix products  42.4 us (7%)
  starting transfers between devices  28 us (5%)
  between operations  24.6 us (4%)
  blocking collectives  16.9 us (3%)
  local copies, waits for them, and re-layouts  16.1 us (3%)
    psum x1, waiting for transfers between devices, broadcast(): return lax.psum(jnp.where(mine, value, jnp.zeros_like(value)), axis)  352 us
    reduce_scatter x3, waiting for transfers between devices, per_device(): lax.psum_scatter(partial_rows(jnp.int32(0), rays_local * lax.axis_size('t...  33.7 us
    dot_general x3, matrix products, add_back(): lax.dot_general(operator_panel, received, (((0,), (0,)), ((), ())), preci...  28.2 us
    ppermute x8, starting transfers between devices, shifted(): return lax.ppermute(value, axis, pairs)  27.9 us
    all_gather x3, blocking collectives, per_device(): lax.all_gather(change, 'tile', axis=0, tiled=True)  16.9 us
    dot_general x3, matrix products, partial_rows(): jnp.dot(operator_panel, estimate, precision=lax.Precision.HIGHEST, prefer...  14.1 us
    mul x4, other arithmetic, primal(): primal_step * penalty * field_div  12.5 us
  transfers between devices with their start and end apart: 12, of which 6 were waited for; matrix products, arithmetic and copies ran while one was open for 8% of the time, Pallas kernels for 0%

commit v1 on v0

v1 whole, which is shorter than its diff:
```python
import jax
import jax.numpy as jnp
from jax import lax
from jax.sharding import PartitionSpec as P

WIDTH = 512
ITERS = 3


penalty = 0.2
smoothing = 1.0

PRECISION = lax.Precision.HIGH


def shifted(value, axis, by):
    count = lax.axis_size(axis)
    pairs = [(i, i + by) for i in range(count) if 0 <= i + by < count]
    return lax.ppermute(value, axis, pairs)


def ring_order(count):
    return list(range(0, count, 2)) + list(range(1, count, 2))[::-1]


def halo(estimate):
    channels = estimate.shape[1]
    image_field = estimate.reshape(-1, WIDTH, channels)
    row_below = shifted(image_field[:1], "tile", -1)
    row_above = shifted(image_field[-1:], "tile", 1)
    return row_below, row_above


def divergence(estimate, halos, tile_index, total_rows):
    channels = estimate.shape[1]
    image_field = estimate.reshape(-1, WIDTH, channels)
    rows_local = image_field.shape[0]
    row_below, row_above = halos
    extended = jnp.concatenate([row_above, image_field, row_below], axis=0)
    current = extended[:-1]
    downward = extended[1:] - current
    global_row = tile_index * rows_local - 1 + lax.broadcasted_iota(jnp.int32, (rows_local + 1, 1, 1), 0)
    inside = (global_row >= 0) & (global_row < total_rows - 1)
    downward = jnp.where(inside, downward, jnp.zeros_like(downward))
    column_zero = jnp.zeros((rows_local + 1, 1, channels), estimate.dtype)
    across = jnp.concatenate([current[:, 1:] - current[:, :-1], column_zero], axis=1)
    magnitude = jnp.sqrt(across * across + downward * downward + smoothing * smoothing)
    flux_across = (across / magnitude)[1:]
    flux_down = downward / magnitude
    shifted_across = jnp.concatenate([column_zero[1:], flux_across[:, :-1]], axis=1)
    field_div = flux_across - shifted_across + flux_down[1:] - flux_down[:-1]
    return field_div.reshape(estimate.shape)


def tile_sum(value):
    count = lax.axis_size("tile")
    step = 1
    while step < count:
        value = value + lax.ppermute(value, "tile", [(i, i ^ step) for i in range(count)])
        step *= 2
    return value


def gather_panels(panels, subset_order):
    count = lax.axis_size("col")
    stored, rays, pixels = panels.shape
    block = rays // count
    order = ring_order(count)
    cw = [(order[i], order[(i + 1) % count]) for i in range(count)]
    ccw = [(b, a) for a, b in cw]
    position_of = [order.index(i) for i in range(count)]
    mine = jnp.asarray(position_of, jnp.int32)[lax.axis_index("col")]
    order = jnp.asarray(order, jnp.int32)

    pieces = panels.reshape(stored, count, block, pixels)
    spread = lax.all_to_all(pieces, "col", split_axis=1, concat_axis=0, tiled=True)
    spread = spread.reshape(count * stored, block, pixels)

    gathered = []
    history = []
    for k in range(ITERS):
        chunk = lax.dynamic_index_in_dim(spread, subset_order[k], 0, keepdims=False)
        if len(history) >= 2:
            chunk, _ = lax.optimization_barrier((chunk, history[-2]))
        whole = jnp.zeros((rays, pixels), jnp.float32)

        def place(whole, piece, distance):
            owner = order[(mine + distance + count) % count]
            return lax.dynamic_update_slice(whole, piece, (owner * block, 0))

        whole = place(whole, chunk, 0)
        forwards, backwards = chunk, chunk
        for step in range(1, count // 2 + 1):
            forwards = lax.ppermute(forwards, "col", cw)
            whole = place(whole, forwards, -step)
            if step < count - step:
                backwards = lax.ppermute(backwards, "col", ccw)
                whole = place(whole, backwards, step)
            history.append((forwards, backwards))
        gathered.append(whole)
    return gathered


def per_device(initial_image, panels, sinogram, subset_order, step_sizes):
    dual_step = step_sizes[0]
    primal_step = step_sizes[1]
    extrapolate = step_sizes[2]
    tile_count = lax.axis_size("tile")
    tile_index = lax.axis_index("tile")
    total_rows = initial_image.shape[0] // WIDTH * tile_count
    rays_local = panels.shape[1] // tile_count
    subset_count = sinogram.shape[0]

    def base_of(estimate):
        field_div = divergence(estimate, halo(estimate), tile_index, total_rows)
        return lax.optimization_barrier(estimate + primal_step * penalty * field_div)

    operator_panels = gather_panels(panels, subset_order)
    measured_own = jnp.stack([lax.dynamic_index_in_dim(sinogram, subset_order[k], 0, keepdims=False) for k in range(ITERS)])
    measured = lax.all_gather(measured_own, "tile", axis=1, tiled=True)

    estimate = base_of(initial_image)
    duals = []
    dual_state = jnp.zeros(sinogram.shape, jnp.float32)
    accumulated = jnp.zeros(initial_image.shape, jnp.float32)
    for k in range(ITERS):
        operator_panel = operator_panels[k]
        forward = tile_sum(
            jnp.dot(operator_panel, estimate, precision=PRECISION, preferred_element_type=jnp.float32)
        )
        base = base_of(estimate)
        current = jnp.zeros_like(forward)
        for j in range(k):
            current = jnp.where(subset_order[j] == subset_order[k], duals[j], current)
        updated = (current + dual_step * forward - dual_step * measured[k]) / (1.0 + dual_step)
        change = updated - current
        duals.append(updated)
        adjoint = lax.dot_general(
            operator_panel,
            change,
            (((0,), (0,)), ((), ())),
            precision=PRECISION,
            preferred_element_type=jnp.float32,
        )
        mine = lax.dynamic_slice_in_dim(updated, tile_index * rays_local, rays_local, 0)
        dual_state = lax.dynamic_update_index_in_dim(dual_state, mine, subset_order[k], 0)
        accumulated = accumulated + adjoint
        extrapolated = accumulated + extrapolate * subset_count * adjoint
        estimate = base - primal_step * extrapolated
    return (estimate, dual_state)


def solution(mesh):
    in_specs = (P("tile", "col"), P("col", None, "tile"), P(None, "tile", "col"), P(), P())
    out_specs = (P("tile", "col"), P(None, "tile", "col"))
    return jax.shard_map(
        per_device, mesh=mesh, in_specs=in_specs, out_specs=out_specs, check_vma=False
    )
```

time: 569 us -> 289 us (0.51); the launches traced: 562 us -> 288 us
  waiting for transfers between devices: 390 us -> 164 us
  other arithmetic: 43.8 us -> 14.6 us
  matrix products: 42.4 us -> 18.3 us
  starting transfers between devices: 28 us -> 46.7 us
  local copies, waits for them, and re-layouts: 16.1 us -> 10.2 us
    psum x1 -> x0, waiting for transfers between devices: 352 us -> none  [broadcast(): return lax.psum(jnp.where(mine, value, jnp.zeros_like(value)), axis)]
    ppermute x0 -> x27, waiting for transfers between devices: none -> 119 us  [the longest x12 101 us: gather_panels(): forwards = lax.ppermute(forwards, 'col', cw)]
    all_to_all x0 -> x1, waiting for transfers between devices: none -> 40.9 us  [gather_panels(): lax.all_to_all(pieces, 'col', split_axis=1, concat_axis=0, tiled=True)]
    reduce_scatter x3 -> x0, waiting for transfers between devices: 33.7 us -> none  [per_device(): lax.psum_scatter(partial_rows(jnp.int32(0), rays_local * lax.axis_size('t...]
    ppermute x0 -> x27, starting transfers between devices: none -> 25.4 us  [the longest x12 11.5 us: gather_panels(): forwards = lax.ppermute(forwards, 'col', cw)]
    dot_general x6, matrix products: 42.4 us -> 18.3 us  [the longest x3 12.7 us: per_device(): lax.dot_general(operator_panel, change, (((0,), (0,)), ((), ())), precisi...]
    ppermute x8, starting transfers between devices: 27.9 us -> 13.9 us  [shifted(): return lax.ppermute(value, axis, pairs)]
    mul x4, other arithmetic: 12.5 us -> 3.11 us  [base_of(): primal_step * penalty * field_div]
  transfers between devices with their start and end apart: 12 -> 36, of which waited for: 6 -> 19; matrix products, arithmetic and copies ran while one was open for 8% -> 11% of each run, Pallas kernels for 0% -> 0%
where the time goes in v1:
time: 289 us; the launch traced here: 288 us
  waiting for transfers between devices  164 us (57%)
  starting transfers between devices  46.7 us (16%)
  between operations  23 us (8%)
  matrix products  18.3 us (6%)
  other arithmetic  14.6 us (5%)
  blocking collectives  11.3 us (4%)
  local copies, waits for them, and re-layouts  10.2 us (4%)
    ppermute x12, waiting for transfers between devices, gather_panels(): forwards = lax.ppermute(forwards, 'col', cw)  101 us
    all_to_all x1, waiting for transfers between devices, gather_panels(): lax.all_to_all(pieces, 'col', split_axis=1, concat_axis=0, tiled=True)  40.9 us
    ppermute x8, starting transfers between devices, shifted(): return lax.ppermute(value, axis, pairs)  13.9 us
    ppermute x6, waiting for transfers between devices, tile_sum(): lax.ppermute(value, 'tile', [(i, i ^ step) for i in range(count)])  13.2 us
    dot_general x3, matrix products, per_device(): lax.dot_general(operator_panel, change, (((0,), (0,)), ((), ())), precisi...  12.7 us
    ppermute x12, starting transfers between devices, gather_panels(): forwards = lax.ppermute(forwards, 'col', cw)  11.5 us
    all_gather x1, blocking collectives, per_device(): measured = lax.all_gather(measured_own, 'tile', axis=1, tiled=True)  11.3 us
    ppermute x9, starting transfers between devices, gather_panels(): backwards = lax.ppermute(backwards, 'col', ccw)  9.81 us
  transfers between devices with their start and end apart: 36, of which 19 were waited for; matrix products, arithmetic and copies ran while one was open for 11% of the time, Pallas kernels for 0%

profile of v1, /device:TPU:0, one launch (start us, length us, event | category | flops | bytes accessed | tf_op | source)
XLA Modules:
  0.0 288.0 jit_solution(13613295664015266008)
XLA Ops:
  0.7 7.4 %all-to-all-start = ((f32[1,8,32,4096]{3,2,0,1:T(8,128)}), f32[1,8,32,4096]{3,2,0,1:T(8,128)}, u32[]{:S(2)}, u32[]{:S(2)}) async-start(f32[1,8,32,4096]{3,2,0,1:T(8,128)} %bitcast.100), calls=%async_computation | async-start | bytes 8388608 | tf_op jit(solution)/shard_map/all_to_all | solution.py:76
  8.2 1.5 collective-permute-start
  9.6 1.3 collective-permute-start.1
  19.4 0.7 fusion.56
  35.2 0.9 constant_dynamic-slice_fusion.2
  36.4 1.3 fusion.27
  38.3 1.1 copy-done.1
  39.7 4.6 %collective-permute-start.2 = (f32[1,512,128]{2,1,0:T(8,128)S(1)}, f32[1,512,128]{2,1,0:T(8,128)S(1)}, u32[]{:S(2)}, u32[]{:S(2)}) collective-permute-start(f32[1,512,128]{2,1,0:T(8,128)S(1)} %get-tuple-element.25), channel_id=1, source_target_pairs={{0,1},{1,2},{2,3},{4,5},{5,6},{6,7},{8,9},{9,10},{10,11},{12,13},{... | collective-permute-start | bytes 786440 | tf_op jit(solution)/shard_map/ppermute | solution.py:19
  44.4 1.3 collective-permute-start.3
  45.7 11.3 %all_gather.3 = f32[3,256,128]{2,1,0:T(8,128)S(1)} all-gather(f32[3,64,128]{2,1,0:T(8,128)S(1)} %pad_maximum_fusion.4), channel_id=1, replica_groups=mesh['col'=8,'tile'=4] {'tile'}, dimensions={1}, use_global_device_ids=true | all-gather | bytes 491520 | tf_op jit(solution)/shard_map/all_gather | solution.py:120
  57.2 1.3 fusion.25
  58.7 1.8 fusion.32
  60.5 40.9 %all-to-all-done = f32[1,8,32,4096]{3,2,0,1:T(8,128)} async-done(((f32[1,8,32,4096]{3,2,0,1:T(8,128)}), f32[1,8,32,4096]{3,2,0,1:T(8,128)}, u32[]{:S(2)}, u32[]{:S(2)}) %all-to-all-start) | async-done | bytes 4194336 | tf_op jit(solution)/shard_map/all_to_all | solution.py:76
  101.9 1.3 constant_dynamic-update-slice_fusion.23
  103.2 2.0 collective-permute-start.5
  105.4 1.3 dynamic-slice_bitcast_fusion
  106.7 9.1 %collective-permute-done.4 = f32[32,4096]{1,0:T(8,128)S(1)} collective-permute-done((f32[32,4096]{1,0:T(8,128)S(1)}, f32[32,4096]{1,0:T(8,128)S(1)}, u32[]{:S(2)}, u32[]{:S(2)}) %collective-permute-start.4) | collective-permute-done | bytes 524320 | tf_op jit(solution)/shard_map/ppermute | solution.py:94
  116.5 1.4 collective-permute-start.7
  118.0 10.0 %collective-permute-done.6 = f32[32,4096]{1,0:T(8,128)S(1)} collective-permute-done((f32[32,4096]{1,0:T(8,128)S(1)}, f32[32,4096]{1,0:T(8,128)S(1)}, u32[]{:S(2)}, u32[]{:S(2)}) %collective-permute-start.6) | collective-permute-done | bytes 524320 | tf_op jit(solution)/shard_map/ppermute | solution.py:94
  127.9 1.0 collective-permute-start.8
  128.9 0.7 collective-permute-done.7
  130.1 9.1 %collective-permute-done.8 = f32[32,4096]{1,0:T(8,128)S(1)} collective-permute-done((f32[32,4096]{1,0:T(8,128)S(1)}, f32[32,4096]{1,0:T(8,128)S(1)}, u32[]{:S(2)}, u32[]{:S(2)}) %collective-permute-start.8) | collective-permute-done | bytes 524320 | tf_op jit(solution)/shard_map/ppermute | solution.py:94
  139.2 2.8 collective-permute-done.9
  142.0 1.6 collective-permute-start.15
  144.0 1.6 collective-permute-start.10
  145.7 19.0 %collective-permute-done.10 = f32[32,4096]{1,0:T(8,128)S(1)} collective-permute-done((f32[32,4096]{1,0:T(8,128)S(1)}, f32[32,4096]{1,0:T(8,128)S(1)}, u32[]{:S(2)}, u32[]{:S(2)}) %collective-permute-start.10) | collective-permute-done | bytes 524320 | tf_op jit(solution)/shard_map/ppermute | solution.py:94
  164.7 1.8 fusion.57
  167.2 1.5 collective-permute-start.17
  168.6 1.6 collective-permute-start.12
  170.3 0.9 collective-permute-start.18
  171.1 3.2 %collective-permute-done.12 = f32[256,128]{1,0:T(8,128)S(1)} collective-permute-done((f32[256,128]{1,0:T(8,128)S(1)}, f32[256,128]{1,0:T(8,128)S(1)}, u32[]{:S(2)}, u32[]{:S(2)}) %collective-permute-start.12) | collective-permute-done | bytes 131104 | tf_op jit(solution)/shard_map/ppermute | solution.py:59
  175.0 3.5 %fusion.58 = f32[4096,128]{1,0:T(8,128)S(1)} fusion(f32[256,4096]{1,0:T(8,128)S(1)} %constant_dynamic-update-slice_fusion.16, f32[256,128]{1,0:T(8,128)S(1)} %fusion.42), kind=kOutput, calls=%fused_computation.138 | convolution fusion | flops 805306368 | bytes 6422528 | tf_op jit(solution)/shard_map/dot_general | solution.py:138
  178.5 1.0 fusion.29
  179.5 1.3 collective-permute-start.13
  180.9 1.3 collective-permute-start.14
  182.5 3.5 %collective-permute-done.14 = f32[1,512,128]{2,1,0:T(8,128)S(1)} collective-permute-done((f32[1,512,128]{2,1,0:T(8,128)S(1)}, f32[1,512,128]{2,1,0:T(8,128)S(1)}, u32[]{:S(2)}, u32[]{:S(2)}) %collective-permute-start.14) | collective-permute-done | bytes 262176 | tf_op jit(solution)/shard_map/ppermute | solution.py:19
  186.1 1.3 fusion.23
  188.2 1.5 collective-permute-start.19
  190.4 8.9 %collective-permute-done.19 = f32[32,4096]{1,0:T(8,128)S(1)} collective-permute-done((f32[32,4096]{1,0:T(8,128)S(1)}, f32[32,4096]{1,0:T(8,128)S(1)}, u32[]{:S(2)}, u32[]{:S(2)}) %collective-permute-start.19) | collective-permute-done | bytes 524320 | tf_op jit(solution)/shard_map/ppermute | solution.py:94
  199.2 1.7 collective-permute-done.20
  201.0 0.7 collective-permute-start.26
  201.7 1.3 collective-permute-start.27
  203.8 20.9 %collective-permute-done.21 = f32[32,4096]{1,0:T(8,128)S(1)} collective-permute-done((f32[32,4096]{1,0:T(8,128)S(1)}, f32[32,4096]{1,0:T(8,128)S(1)}, u32[]{:S(2)}, u32[]{:S(2)}) %collective-permute-start.21) | collective-permute-done | bytes 524320 | tf_op jit(solution)/shard_map/ppermute | solution.py:94
  224.7 1.9 fusion.59
  226.6 2.3 collective-permute-start.22
  229.4 0.7 collective-permute-start.28
  230.3 1.6 collective-permute-start.29
  231.9 3.8 %collective-permute-done.23 = f32[256,128]{1,0:T(8,128)S(1)} collective-permute-done((f32[256,128]{1,0:T(8,128)S(1)}, f32[256,128]{1,0:T(8,128)S(1)}, u32[]{:S(2)}, u32[]{:S(2)}) %collective-permute-start.23) | collective-permute-done | bytes 131104 | tf_op jit(solution)/shard_map/ppermute | solution.py:59
  235.7 0.7 fusion.39
  236.3 3.5 %fusion.47 = f32[4096,128]{1,0:T(8,128)S(1)} fusion(f32[256,4096]{1,0:T(8,128)S(1)} %constant_dynamic-update-slice_fusion.8, f32[256,128]{1,0:T(8,128)S(1)} %fusion.39, f32[256,128]{1,0:T(8,128)S(1)} %fusion.42, pred[]{:T(512)S(6)} %eq.34), kind=kOutput, calls=%fused_computation.95 | convolution fusion | flops 805371904 | bytes 6553601 | tf_op jit(solution)/shard_map/dot_general | solution.py:138
  239.9 1.2 multiply_subtract_fusion.1
  241.2 1.3 collective-permute-start.24
  242.5 1.3 collective-permute-start.25
  243.9 0.8 collective-permute-start.30
  244.7 1.3 collective-permute-start.31
  246.5 1.3 fusion.21
  248.0 10.0 %collective-permute-done.30 = f32[32,4096]{1,0:T(8,128)S(1)} collective-permute-done((f32[32,4096]{1,0:T(8,128)S(1)}, f32[32,4096]{1,0:T(8,128)S(1)}, u32[]{:S(2)}, u32[]{:S(2)}) %collective-permute-start.30) | collective-permute-done | bytes 524320 | tf_op jit(solution)/shard_map/ppermute | solution.py:94
  258.1 0.7 collective-permute-start.32
  259.1 13.5 %collective-permute-done.32 = f32[32,4096]{1,0:T(8,128)S(1)} collective-permute-done((f32[32,4096]{1,0:T(8,128)S(1)}, f32[32,4096]{1,0:T(8,128)S(1)}, u32[]{:S(2)}, u32[]{:S(2)}) %collective-permute-start.32) | collective-permute-done | bytes 524320 | tf_op jit(solution)/shard_map/ppermute | solution.py:94
  272.7 1.9 fusion.60
  275.1 0.9 collective-permute-done.33
  276.3 5.3 %collective-permute-done.34 = f32[256,128]{1,0:T(8,128)S(1)} collective-permute-done((f32[256,128]{1,0:T(8,128)S(1)}, f32[256,128]{1,0:T(8,128)S(1)}, u32[]{:S(2)}, u32[]{:S(2)}) %collective-permute-start.34) | collective-permute-done | bytes 131104 | tf_op jit(solution)/shard_map/ppermute | solution.py:59
  281.6 0.7 fusion.36
  282.3 5.7 %multiply_subtract_fusion = f32[4096,128]{1,0:T(8,128)} fusion(f32[4096,128]{1,0:T(8,128)S(1)} %bitcast_add_fusion, f32[4096,128]{1,0:T(8,128)S(1)} %get-tuple-element.7, f32[]{:T(128)} %bitcast.32, f32[]{:T(128)} %bitcast, f32[256,4096]{1,0:T(8,128)S(1)} %constant_dynamic-update-slice_fusion, f32[256,128]{1,0:T(8,128)S(1)} %fusion.36, ...), kind=kOutput, calls=%fused_computation.67 | convolution fusion | flops 808026112 | bytes 10878986 | tf_op jit(solution)/shard_map/dot_general | solution.py:138
  (102 shorter events, 12.5 us)
Async XLA Ops:
  0.6 7.5 %copy-start = (f32[4096,128]{1,0:T(8,128)S(1)}, f32[4096,128]{1,0:T(8,128)}, u32[]{:S(2)}) copy-start(f32[4096,128]{1,0:T(8,128)} %param.7) | copy-start | bytes 6291460
  0.6 10.3 %copy-start.5 = (f32[3]{0:T(128)S(1)}, f32[3]{0:T(128)}, u32[]{:S(2)}) copy-start(f32[3]{0:T(128)} %param.11) | copy-start | bytes 40
  0.7 11.0 %copy-start.6 = (s32[3]{0:T(128)S(1)}, s32[3]{0:T(128)}, u32[]{:S(2)}) copy-start(s32[3]{0:T(128)} %param.10) | copy-start | bytes 40
  0.7 11.6 %copy-start.7 = (s32[8]{0:T(128)S(1)}, s32[8]{0:T(128)}, u32[]{:S(2)}) copy-start(s32[8]{0:T(128)} %constant.178.clone) | copy-start | bytes 100
  0.7 18.8 %copy-start.4 = (s32[8]{0:T(128)S(1)}, s32[8]{0:T(128)}, u32[]{:S(2)}) copy-start(s32[8]{0:T(128)} %constant.179.clone) | copy-start | bytes 100
  0.7 100.7 %all-to-all-start = ((f32[1,8,32,4096]{3,2,0,1:T(8,128)}), f32[1,8,32,4096]{3,2,0,1:T(8,128)}, u32[]{:S(2)}, u32[]{:S(2)}) async-start(f32[1,8,32,4096]{3,2,0,1:T(8,128)} %bitcast.100), calls=%async_computation | async-start | bytes 8388608 | tf_op jit(solution)/shard_map/all_to_all | solution.py:76
  8.2 27.9 %collective-permute-start = (f32[1,512,128]{2,1,0:T(8,128)S(1)}, f32[1,512,128]{2,1,0:T(8,128)S(1)}, u32[]{:S(2)}, u32[]{:S(2)}) collective-permute-start(f32[1,512,128]{2,1,0:T(8,128)S(1)} %get-tuple-element.27), channel_id=1, source_target_pairs={{0,1},{1,2},{2,3},{4,5},{5,6},{6,7},{8,9},{9,10},{10,11},{12,13},{... | collective-permute-start | bytes 786440 | tf_op jit(solution)/shard_map/ppermute | solution.py:19
  9.6 26.7 %collective-permute-start.1 = (f32[1,512,128]{2,1,0:T(8,128)S(1)}, f32[1,512,128]{2,1,0:T(8,128)S(1)}, u32[]{:S(2)}, u32[]{:S(2)}) collective-permute-start(f32[1,512,128]{2,1,0:T(8,128)S(1)} %get-tuple-element.26), channel_id=1, source_target_pairs={{1,0},{2,1},{3,2},{5,4},{6,5},{7,6},{9,8},{10,9},{11,10},{13,12},{... | collective-permute-start | bytes 786440 | tf_op jit(solution)/shard_map/ppermute | solution.py:19
  37.8 1.6 copy-start.1
  39.7 17.2 %collective-permute-start.2 = (f32[1,512,128]{2,1,0:T(8,128)S(1)}, f32[1,512,128]{2,1,0:T(8,128)S(1)}, u32[]{:S(2)}, u32[]{:S(2)}) collective-permute-start(f32[1,512,128]{2,1,0:T(8,128)S(1)} %get-tuple-element.25), channel_id=1, source_target_pairs={{0,1},{1,2},{2,3},{4,5},{5,6},{6,7},{8,9},{9,10},{10,11},{12,13},{... | collective-permute-start | bytes 786440 | tf_op jit(solution)/shard_map/ppermute | solution.py:19
  44.4 12.8 %collective-permute-start.3 = (f32[1,512,128]{2,1,0:T(8,128)S(1)}, f32[1,512,128]{2,1,0:T(8,128)S(1)}, u32[]{:S(2)}, u32[]{:S(2)}) collective-permute-start(f32[1,512,128]{2,1,0:T(8,128)S(1)} %get-tuple-element.24), channel_id=1, source_target_pairs={{1,0},{2,1},{3,2},{5,4},{6,5},{7,6},{9,8},{10,9},{11,10},{13,12},{... | collective-permute-start | bytes 786440 | tf_op jit(solution)/shard_map/ppermute | solution.py:19
  101.4 3.8 %copy-start.2 = (f32[8,512,128]{2,1,0:T(8,128)S(1)}, f32[8,512,128]{2,1,0:T(8,128)}, u32[]{:S(2)}) copy-start(f32[8,512,128]{2,1,0:T(8,128)} %fusion.32) | copy-start | bytes 6291460
  103.1 12.7 %collective-permute-start.4 = (f32[32,4096]{1,0:T(8,128)S(1)}, f32[32,4096]{1,0:T(8,128)S(1)}, u32[]{:S(2)}, u32[]{:S(2)}) collective-permute-start(f32[32,4096]{1,0:T(8,128)S(1)} %get-tuple-element.9), channel_id=1, source_target_pairs={{0,8},{8,16},{16,24},{24,28},{28,20},{20,12},{12,4},{4,0},{1,9},{9... | collective-permute-start | bytes 1572872 | tf_op jit(solution)/shard_map/ppermute | solution.py:94
  103.2 13.3 %collective-permute-start.5 = (f32[32,4096]{1,0:T(8,128)S(1)}, f32[32,4096]{1,0:T(8,128)S(1)}, u32[]{:S(2)}, u32[]{:S(2)}) collective-permute-start(f32[32,4096]{1,0:T(8,128)S(1)} %get-tuple-element.9), channel_id=1, source_target_pairs={{8,0},{16,8},{24,16},{28,24},{20,28},{12,20},{4,12},{0,4},{9,1},{1... | collective-permute-start | bytes 1572872 | tf_op jit(solution)/shard_map/ppermute | solution.py:97
  115.9 12.1 %collective-permute-start.6 = (f32[32,4096]{1,0:T(8,128)S(1)}, f32[32,4096]{1,0:T(8,128)S(1)}, u32[]{:S(2)}, u32[]{:S(2)}) collective-permute-start(f32[32,4096]{1,0:T(8,128)S(1)} %collective-permute-done.4), channel_id=1, source_target_pairs={{0,8},{8,16},{16,24},{24,28},{28,20},{20,12},{12,4},{4,0},{1,9},{9... | collective-permute-start | bytes 1572872 | tf_op jit(solution)/shard_map/ppermute | solution.py:94
  116.5 13.2 %collective-permute-start.7 = (f32[32,4096]{1,0:T(8,128)S(1)}, f32[32,4096]{1,0:T(8,128)S(1)}, u32[]{:S(2)}, u32[]{:S(2)}) collective-permute-start(f32[32,4096]{1,0:T(8,128)S(1)} %collective-permute-done.5), channel_id=1, source_target_pairs={{8,0},{16,8},{24,16},{28,24},{20,28},{12,20},{4,12},{0,4},{9,1},{1... | collective-permute-start | bytes 1572872 | tf_op jit(solution)/shard_map/ppermute | solution.py:97
  127.9 11.2 %collective-permute-start.8 = (f32[32,4096]{1,0:T(8,128)S(1)}, f32[32,4096]{1,0:T(8,128)S(1)}, u32[]{:S(2)}, u32[]{:S(2)}) collective-permute-start(f32[32,4096]{1,0:T(8,128)S(1)} %collective-permute-done.6), channel_id=1, source_target_pairs={{0,8},{8,16},{16,24},{24,28},{28,20},{20,12},{12,4},{4,0},{1,9},{9... | collective-permute-start | bytes 1572872 | tf_op jit(solution)/shard_map/ppermute | solution.py:94
  129.7 12.3 %collective-permute-start.9 = (f32[32,4096]{1,0:T(8,128)S(1)}, f32[32,4096]{1,0:T(8,128)S(1)}, u32[]{:S(2)}, u32[]{:S(2)}) collective-permute-start(f32[32,4096]{1,0:T(8,128)S(1)} %collective-permute-done.7), channel_id=1, source_target_pairs={{8,0},{16,8},{24,16},{28,24},{20,28},{12,20},{4,12},{0,4},{9,1},{1... | collective-permute-start | bytes 1572872 | tf_op jit(solution)/shard_map/ppermute | solution.py:97
  142.0 25.2 %collective-permute-start.15 = (f32[32,4096]{1,0:T(8,128)S(1)}, f32[32,4096]{1,0:T(8,128)S(1)}, u32[]{:S(2)}, u32[]{:S(2)}) collective-permute-start(f32[32,4096]{1,0:T(8,128)S(1)} %get-tuple-element.4), channel_id=1, source_target_pairs={{0,8},{8,16},{16,24},{24,28},{28,20},{20,12},{12,4},{4,0},{1,9},{9... | collective-permute-start | bytes 1572872 | tf_op jit(solution)/shard_map/ppermute | solution.py:94
  143.5 26.7 %collective-permute-start.16 = (f32[32,4096]{1,0:T(8,128)S(1)}, f32[32,4096]{1,0:T(8,128)S(1)}, u32[]{:S(2)}, u32[]{:S(2)}) collective-permute-start(f32[32,4096]{1,0:T(8,128)S(1)} %get-tuple-element.4), channel_id=1, source_target_pairs={{8,0},{16,8},{24,16},{28,24},{20,28},{12,20},{4,12},{0,4},{9,1},{1... | collective-permute-start | bytes 1572872 | tf_op jit(solution)/shard_map/ppermute | solution.py:97
  144.0 20.7 %collective-permute-start.10 = (f32[32,4096]{1,0:T(8,128)S(1)}, f32[32,4096]{1,0:T(8,128)S(1)}, u32[]{:S(2)}, u32[]{:S(2)}) collective-permute-start(f32[32,4096]{1,0:T(8,128)S(1)} %collective-permute-done.8), channel_id=1, source_target_pairs={{0,8},{8,16},{16,24},{24,28},{28,20},{20,12},{12,4},{4,0},{1,9},{9... | collective-permute-start | bytes 1572872 | tf_op jit(solution)/shard_map/ppermute | solution.py:94
  166.5 2.1 collective-permute-start.11
  167.2 21.0 %collective-permute-start.17 = (f32[32,4096]{1,0:T(8,128)S(1)}, f32[32,4096]{1,0:T(8,128)S(1)}, u32[]{:S(2)}, u32[]{:S(2)}) collective-permute-start(f32[32,4096]{1,0:T(8,128)S(1)} %collective-permute-done.15), channel_id=1, source_target_pairs={{0,8},{8,16},{16,24},{24,28},{28,20},{20,12},{12,4},{4,0},{1,9},{9... | collective-permute-start | bytes 1572872 | tf_op jit(solution)/shard_map/ppermute | solution.py:94
  168.6 5.7 %collective-permute-start.12 = (f32[256,128]{1,0:T(8,128)S(1)}, f32[256,128]{1,0:T(8,128)S(1)}, u32[]{:S(2)}, u32[]{:S(2)}) collective-permute-start(f32[256,128]{1,0:T(8,128)S(1)} %add.424), channel_id=1, source_target_pairs={{0,2},{1,3},{2,0},{3,1},{4,6},{5,7},{6,4},{7,5},{8,10},{9,11},{10,... | collective-permute-start | bytes 393224 | tf_op jit(solution)/shard_map/ppermute | solution.py:59
  170.3 19.4 %collective-permute-start.18 = (f32[32,4096]{1,0:T(8,128)S(1)}, f32[32,4096]{1,0:T(8,128)S(1)}, u32[]{:S(2)}, u32[]{:S(2)}) collective-permute-start(f32[32,4096]{1,0:T(8,128)S(1)} %collective-permute-done.16), channel_id=1, source_target_pairs={{8,0},{16,8},{24,16},{28,24},{20,28},{12,20},{4,12},{0,4},{9,1},{1... | collective-permute-start | bytes 1572872 | tf_op jit(solution)/shard_map/ppermute | solution.py:97
  179.5 2.7 collective-permute-start.13
  180.9 5.2 %collective-permute-start.14 = (f32[1,512,128]{2,1,0:T(8,128)S(1)}, f32[1,512,128]{2,1,0:T(8,128)S(1)}, u32[]{:S(2)}, u32[]{:S(2)}) collective-permute-start(f32[1,512,128]{2,1,0:T(8,128)S(1)} %get-tuple-element.22), channel_id=1, source_target_pairs={{1,0},{2,1},{3,2},{5,4},{6,5},{7,6},{9,8},{10,9},{11,10},{13,12},{... | collective-permute-start | bytes 786440 | tf_op jit(solution)/shard_map/ppermute | solution.py:19
  188.2 11.1 %collective-permute-start.19 = (f32[32,4096]{1,0:T(8,128)S(1)}, f32[32,4096]{1,0:T(8,128)S(1)}, u32[]{:S(2)}, u32[]{:S(2)}) collective-permute-start(f32[32,4096]{1,0:T(8,128)S(1)} %collective-permute-done.17), channel_id=1, source_target_pairs={{0,8},{8,16},{16,24},{24,28},{28,20},{20,12},{12,4},{4,0},{1,9},{9... | collective-permute-start | bytes 1572872 | tf_op jit(solution)/shard_map/ppermute | solution.py:94
  189.7 11.3 %collective-permute-start.20 = (f32[32,4096]{1,0:T(8,128)S(1)}, f32[32,4096]{1,0:T(8,128)S(1)}, u32[]{:S(2)}, u32[]{:S(2)}) collective-permute-start(f32[32,4096]{1,0:T(8,128)S(1)} %collective-permute-done.18), channel_id=1, source_target_pairs={{8,0},{16,8},{24,16},{28,24},{20,28},{12,20},{4,12},{0,4},{9,1},{1... | collective-permute-start | bytes 1572872 | tf_op jit(solution)/shard_map/ppermute | solution.py:97
  201.0 28.4 %collective-permute-start.26 = (f32[32,4096]{1,0:T(8,128)S(1)}, f32[32,4096]{1,0:T(8,128)S(1)}, u32[]{:S(2)}, u32[]{:S(2)}) collective-permute-start(f32[32,4096]{1,0:T(8,128)S(1)} %get-tuple-element.5), channel_id=1, source_target_pairs={{0,8},{8,16},{16,24},{24,28},{28,20},{20,12},{12,4},{4,0},{1,9},{9... | collective-permute-start | bytes 1572872 | tf_op jit(solution)/shard_map/ppermute | solution.py:94
  201.7 28.6 %collective-permute-start.27 = (f32[32,4096]{1,0:T(8,128)S(1)}, f32[32,4096]{1,0:T(8,128)S(1)}, u32[]{:S(2)}, u32[]{:S(2)}) collective-permute-start(f32[32,4096]{1,0:T(8,128)S(1)} %get-tuple-element.5), channel_id=1, source_target_pairs={{8,0},{16,8},{24,16},{28,24},{20,28},{12,20},{4,12},{0,4},{9,1},{1... | collective-permute-start | bytes 1572872 | tf_op jit(solution)/shard_map/ppermute | solution.py:97
  203.0 21.6 %collective-permute-start.21 = (f32[32,4096]{1,0:T(8,128)S(1)}, f32[32,4096]{1,0:T(8,128)S(1)}, u32[]{:S(2)}, u32[]{:S(2)}) collective-permute-start(f32[32,4096]{1,0:T(8,128)S(1)} %collective-permute-done.19), channel_id=1, source_target_pairs={{0,8},{8,16},{16,24},{24,28},{28,20},{20,12},{12,4},{4,0},{1,9},{9... | collective-permute-start | bytes 1572872 | tf_op jit(solution)/shard_map/ppermute | solution.py:94
  226.6 3.5 %collective-permute-start.22 = (f32[256,128]{1,0:T(8,128)S(1)}, f32[256,128]{1,0:T(8,128)S(1)}, u32[]{:S(2)}, u32[]{:S(2)}) collective-permute-start(f32[256,128]{1,0:T(8,128)S(1)} %fusion.59), channel_id=1, source_target_pairs={{0,1},{1,0},{2,3},{3,2},{4,5},{5,4},{6,7},{7,6},{8,9},{9,8},{10,11... | collective-permute-start | bytes 393224 | tf_op jit(solution)/shard_map/ppermute | solution.py:59
  229.4 14.5 %collective-permute-start.28 = (f32[32,4096]{1,0:T(8,128)S(1)}, f32[32,4096]{1,0:T(8,128)S(1)}, u32[]{:S(2)}, u32[]{:S(2)}) collective-permute-start(f32[32,4096]{1,0:T(8,128)S(1)} %collective-permute-done.26), channel_id=1, source_target_pairs={{0,8},{8,16},{16,24},{24,28},{28,20},{20,12},{12,4},{4,0},{1,9},{9... | collective-permute-start | bytes 1572872 | tf_op jit(solution)/shard_map/ppermute | solution.py:94
  230.1 5.6 %collective-permute-start.23 = (f32[256,128]{1,0:T(8,128)S(1)}, f32[256,128]{1,0:T(8,128)S(1)}, u32[]{:S(2)}, u32[]{:S(2)}) collective-permute-start(f32[256,128]{1,0:T(8,128)S(1)} %add.434), channel_id=1, source_target_pairs={{0,2},{1,3},{2,0},{3,1},{4,6},{5,7},{6,4},{7,5},{8,10},{9,11},{10,... | collective-permute-start | bytes 393224 | tf_op jit(solution)/shard_map/ppermute | solution.py:59
  230.3 14.4 %collective-permute-start.29 = (f32[32,4096]{1,0:T(8,128)S(1)}, f32[32,4096]{1,0:T(8,128)S(1)}, u32[]{:S(2)}, u32[]{:S(2)}) collective-permute-start(f32[32,4096]{1,0:T(8,128)S(1)} %collective-permute-done.27), channel_id=1, source_target_pairs={{8,0},{16,8},{24,16},{28,24},{20,28},{12,20},{4,12},{0,4},{9,1},{1... | collective-permute-start | bytes 1572872 | tf_op jit(solution)/shard_map/ppermute | solution.py:97
  241.2 4.8 %collective-permute-start.24 = (f32[1,512,128]{2,1,0:T(8,128)S(1)}, f32[1,512,128]{2,1,0:T(8,128)S(1)}, u32[]{:S(2)}, u32[]{:S(2)}) collective-permute-start(f32[1,512,128]{2,1,0:T(8,128)S(1)} %get-tuple-element.21), channel_id=1, source_target_pairs={{0,1},{1,2},{2,3},{4,5},{5,6},{6,7},{8,9},{9,10},{10,11},{12,13},{... | collective-permute-start | bytes 786440 | tf_op jit(solution)/shard_map/ppermute | solution.py:19
  242.5 3.9 %collective-permute-start.25 = (f32[1,512,128]{2,1,0:T(8,128)S(1)}, f32[1,512,128]{2,1,0:T(8,128)S(1)}, u32[]{:S(2)}, u32[]{:S(2)}) collective-permute-start(f32[1,512,128]{2,1,0:T(8,128)S(1)} %get-tuple-element.20), channel_id=1, source_target_pairs={{1,0},{2,1},{3,2},{5,4},{6,5},{7,6},{9,8},{10,9},{11,10},{13,12},{... | collective-permute-start | bytes 786440 | tf_op jit(solution)/shard_map/ppermute | solution.py:19
  243.9 14.2 %collective-permute-start.30 = (f32[32,4096]{1,0:T(8,128)S(1)}, f32[32,4096]{1,0:T(8,128)S(1)}, u32[]{:S(2)}, u32[]{:S(2)}) collective-permute-start(f32[32,4096]{1,0:T(8,128)S(1)} %collective-permute-done.28), channel_id=1, source_target_pairs={{0,8},{8,16},{16,24},{24,28},{28,20},{20,12},{12,4},{4,0},{1,9},{9... | collective-permute-start | bytes 1572872 | tf_op jit(solution)/shard_map/ppermute | solution.py:94
  244.7 14.4 %collective-permute-start.31 = (f32[32,4096]{1,0:T(8,128)S(1)}, f32[32,4096]{1,0:T(8,128)S(1)}, u32[]{:S(2)}, u32[]{:S(2)}) collective-permute-start(f32[32,4096]{1,0:T(8,128)S(1)} %collective-permute-done.29), channel_id=1, source_target_pairs={{8,0},{16,8},{24,16},{28,24},{20,28},{12,20},{4,12},{0,4},{9,1},{1... | collective-permute-start | bytes 1572872 | tf_op jit(solution)/shard_map/ppermute | solution.py:97
  258.1 14.6 %collective-permute-start.32 = (f32[32,4096]{1,0:T(8,128)S(1)}, f32[32,4096]{1,0:T(8,128)S(1)}, u32[]{:S(2)}, u32[]{:S(2)}) collective-permute-start(f32[32,4096]{1,0:T(8,128)S(1)} %collective-permute-done.30), channel_id=1, source_target_pairs={{0,8},{8,16},{16,24},{24,28},{28,20},{20,12},{12,4},{4,0},{1,9},{9... | collective-permute-start | bytes 1572872 | tf_op jit(solution)/shard_map/ppermute | solution.py:94
  274.6 1.4 collective-permute-start.33
  276.0 5.6 %collective-permute-start.34 = (f32[256,128]{1,0:T(8,128)S(1)}, f32[256,128]{1,0:T(8,128)S(1)}, u32[]{:S(2)}, u32[]{:S(2)}) collective-permute-start(f32[256,128]{1,0:T(8,128)S(1)} %add.443), channel_id=1, source_target_pairs={{0,2},{1,3},{2,0},{3,1},{4,6},{5,7},{6,4},{7,5},{8,10},{9,11},{10,... | collective-permute-start | bytes 393224 | tf_op jit(solution)/shard_map/ppermute | solution.py:59
  282.3 5.7 %copy-start.3 = (f32[8,64,128]{2,1,0:T(8,128)}, f32[8,64,128]{2,1,0:T(8,128)S(1)}, u32[]{:S(2)}) copy-start(f32[8,64,128]{2,1,0:T(8,128)S(1)} %bitcast_dynamic-update-slice_fusion) | copy-start | bytes 786436

commit v2 on v1

v2 whole, which is shorter than its diff:
```python
import jax
import jax.numpy as jnp
from jax import lax
from jax.sharding import PartitionSpec as P


WIDTH = 512
ITERS = 3


penalty = 0.2
smoothing = 1.0

PRECISION = lax.Precision.HIGH
PIECES = 4


def shifted(value, axis, by):
    count = lax.axis_size(axis)
    pairs = [(i, i + by) for i in range(count) if 0 <= i + by < count]
    return lax.ppermute(value, axis, pairs)


def halo(estimate):
    channels = estimate.shape[1]
    image_field = estimate.reshape(-1, WIDTH, channels)
    row_below = shifted(image_field[:1], "tile", -1)
    row_above = shifted(image_field[-1:], "tile", 1)
    return row_below, row_above


def divergence(estimate, halos, tile_index, total_rows):
    channels = estimate.shape[1]
    image_field = estimate.reshape(-1, WIDTH, channels)
    rows_local = image_field.shape[0]
    row_below, row_above = halos
    extended = jnp.concatenate([row_above, image_field, row_below], axis=0)
    current = extended[:-1]
    downward = extended[1:] - current
    global_row = tile_index * rows_local - 1 + lax.broadcasted_iota(jnp.int32, (rows_local + 1, 1, 1), 0)
    inside = (global_row >= 0) & (global_row < total_rows - 1)
    downward = jnp.where(inside, downward, jnp.zeros_like(downward))
    column_zero = jnp.zeros((rows_local + 1, 1, channels), estimate.dtype)
    across = jnp.concatenate([current[:, 1:] - current[:, :-1], column_zero], axis=1)
    magnitude = jnp.sqrt(across * across + downward * downward + smoothing * smoothing)
    flux_across = (across / magnitude)[1:]
    flux_down = downward / magnitude
    shifted_across = jnp.concatenate([column_zero[1:], flux_across[:, :-1]], axis=1)
    field_div = flux_across - shifted_across + flux_down[1:] - flux_down[:-1]
    return field_div.reshape(estimate.shape)


def tile_sum(value):
    count = lax.axis_size("tile")
    step = 1
    while step < count:
        value = value + lax.ppermute(value, "tile", [(i, i ^ step) for i in range(count)])
        step *= 2
    return value


def exchange(value, bit):
    count = lax.axis_size("col")
    return lax.ppermute(value, "col", [(i, i ^ bit) for i in range(count)])


def block_bits(group):
    bits = []
    bit = group // 2
    while bit:
        bits.append(bit)
        bit //= 2
    return bits


def to_arrival_order(rows, group, mine, axis):
    lead = rows.shape[:axis]
    tail = rows.shape[axis + 1 :]
    bits = block_bits(group)
    block = rows.shape[axis] // group
    rows = rows.reshape(lead + (2,) * len(bits) + (PIECES, block // PIECES) + tail)
    for at, bit in enumerate(bits):
        flip = (mine & bit) != 0
        rows = jnp.where(flip, jnp.flip(rows, axis + at), rows)
    order = list(range(axis))
    order += [axis + len(bits)]
    order += [axis + at for at in reversed(range(len(bits)))]
    order += list(range(axis + len(bits) + 1, rows.ndim))
    return rows.transpose(order).reshape(lead + (-1,) + tail)


def from_arrival_order(rows, group, mine):
    tail = rows.shape[1:]
    bits = block_bits(group)
    total = rows.shape[0]
    rows = rows.reshape((PIECES,) + (2,) * len(bits) + (total // group // PIECES,) + tail)
    order = [1 + at for at in reversed(range(len(bits)))] + [0]
    order += list(range(len(bits) + 1, rows.ndim))
    rows = rows.transpose(order)
    for at, bit in enumerate(bits):
        flip = (mine & bit) != 0
        rows = jnp.where(flip, jnp.flip(rows, at), rows)
    return rows.reshape((total,) + tail)


def spread_panels(panels, group):
    stored, rays, pixels = panels.shape
    sub = rays // group // PIECES
    mine = lax.axis_index("col") & (group - 1)
    spread = []
    for piece in range(PIECES):
        blocks = panels.reshape(stored, group, PIECES, sub, pixels)
        parts = [
            lax.dynamic_slice(
                blocks, (0, mine ^ bit, piece, 0, 0), (stored, 1, 1, sub, pixels), allow_negative_indices=False
            ).reshape(stored, sub, pixels)
            for bit in range(group)
        ]
        parts, panels = lax.optimization_barrier((parts, panels))
        for bit in range(1, group):
            parts[bit] = exchange(parts[bit], bit)
        spread.append(parts)
    return spread


def choose(parts, wanted, local):
    near = None
    for bit, part in enumerate(parts):
        held = part[0]
        for at in range(1, part.shape[0]):
            held = jnp.where(local == at, part[at], held)
        near = held if near is None else jnp.where(wanted == bit, held, near)
    return near


def rows_of(values, width):
    return lax.optimization_barrier(jnp.broadcast_to(values.reshape(-1, 1), (values.size, width)))


def gather_panels(panels, subset_order):
    group = lax.axis_size("col") // 2
    stored, _, pixels = panels.shape
    me = lax.axis_index("col")
    spread = spread_panels(panels, group)
    bits = block_bits(group)
    owner = rows_of(lax.div(subset_order, jnp.int32(stored)) ^ me, pixels)
    local = rows_of(lax.rem(subset_order, jnp.int32(stored)), pixels) if stored > 1 else None
    arrived = []
    for k in range(ITERS):
        distance = owner[k : k + 1]
        place = None if local is None else local[k : k + 1]
        for piece in range(PIECES):
            parts, apart = lax.optimization_barrier((spread[piece], distance))
            near = choose(parts, apart & (group - 1), place)
            near, apart = lax.optimization_barrier((near, distance))
            far = exchange(near, group)
            known = jnp.where(apart < group, near, far)
            known = lax.optimization_barrier(known)
            parts = [known]
            for at, bit in enumerate(bits):
                other = exchange(known, bit)
                parts.append(other)
                if at + 1 < len(bits):
                    known = jnp.concatenate([known, other], axis=0)
                    known = lax.optimization_barrier(known)
            arrived.append(parts)
    gathered = []
    for k in range(ITERS):
        parts = sum(arrived[k * PIECES : (k + 1) * PIECES], [])
        gathered.append(jnp.concatenate(lax.optimization_barrier(parts), axis=0))
    return gathered


def per_device(initial_image, panels, sinogram, subset_order, step_sizes):
    channels = initial_image.shape[1]
    dual_step, primal_step, extrapolate = jnp.split(rows_of(step_sizes, channels), 3)
    chosen = [row[None] for row in jnp.split(rows_of(subset_order, channels), ITERS)]
    tile_count = lax.axis_size("tile")
    tile_index = lax.axis_index("tile")
    total_rows = initial_image.shape[0] // WIDTH * tile_count
    rays_local = panels.shape[1] // tile_count
    subset_count = sinogram.shape[0]
    group = lax.axis_size("col") // 2
    mine = lax.axis_index("col") & (group - 1)

    def base_of(estimate):
        field_div = divergence(estimate, halo(estimate), tile_index, total_rows)
        return lax.optimization_barrier(estimate + primal_step * penalty * field_div)

    operator_panels = gather_panels(panels, subset_order)
    subset_at = lax.broadcasted_iota(jnp.int32, (subset_count, 1, 1), 0)
    measured = jnp.stack([jnp.sum(jnp.where(subset_at == chosen[k], sinogram, 0.0), axis=0) for k in range(ITERS)])
    everywhere = jnp.zeros((ITERS, panels.shape[1], sinogram.shape[2]), jnp.float32)
    measured = lax.dynamic_update_slice(everywhere, measured, (0, tile_index * rays_local, 0), allow_negative_indices=False)
    measured = to_arrival_order(measured, group, mine, 1)

    estimate = base_of(initial_image)
    duals = []
    dual_state = jnp.zeros(sinogram.shape, jnp.float32)
    accumulated = jnp.zeros(initial_image.shape, jnp.float32)
    for k in range(ITERS):
        operator_panel = operator_panels[k]
        residual = tile_sum(
            jnp.dot(operator_panel, estimate, precision=PRECISION, preferred_element_type=jnp.float32)
            - measured[k]
        )
        base = base_of(estimate)
        current = jnp.zeros_like(residual)
        for j in range(k):
            current = jnp.where(chosen[j][0] == chosen[k][0], duals[j], current)
        updated = (current + dual_step * residual) / (1.0 + dual_step)
        change = updated - current
        duals.append(updated)
        adjoint = lax.dot_general(
            operator_panel,
            change,
            (((0,), (0,)), ((), ())),
            precision=PRECISION,
            preferred_element_type=jnp.float32,
        )
        ordered = from_arrival_order(updated, group, mine)
        own_rays = lax.dynamic_slice_in_dim(ordered, tile_index * rays_local, rays_local, 0, allow_negative_indices=False)
        dual_state = jnp.where(subset_at == chosen[k], own_rays[None], dual_state)
        accumulated = accumulated + adjoint
        extrapolated = accumulated + extrapolate * subset_count * adjoint
        estimate = base - primal_step * extrapolated
    return (estimate, dual_state)


def solution(mesh):
    in_specs = (P("tile", "col"), P("col", None, "tile"), P(None, "tile", "col"), P(), P())
    out_specs = (P("tile", "col"), P(None, "tile", "col"))

    return jax.shard_map(per_device, mesh=mesh, in_specs=in_specs, out_specs=out_specs, check_vma=False)
```

time: 289 us -> 435 us (1.51); the launches traced: 288 us -> 429 us
  waiting for transfers between devices: 164 us -> 289 us
  starting transfers between devices: 46.7 us -> 82.3 us
  between operations: 23 us -> 1.88 us
  blocking collectives: 11.3 us -> 0 us
  other arithmetic: 14.6 us -> 23.8 us
  local copies, waits for them, and re-layouts: 10.2 us -> 15.1 us
    ppermute x21 -> x48, waiting for transfers between devices: 106 us -> 275 us  [exchange(): return lax.ppermute(value, 'col', [(i, i ^ bit) for i in range(count)])]
    all_to_all x1 -> x0, waiting for transfers between devices: 40.9 us -> none  [gather_panels(): lax.all_to_all(pieces, 'col', split_axis=1, concat_axis=0, tiled=True)]
    ppermute x21 -> x48, starting transfers between devices: 21.3 us -> 60.9 us  [exchange(): return lax.ppermute(value, 'col', [(i, i ^ bit) for i in range(count)])]
    all_gather x1 -> x0, blocking collectives: 11.3 us -> none  [per_device(): measured = lax.all_gather(measured_own, 'tile', axis=1, tiled=True)]
    select_n x0 -> x32, other arithmetic: none -> 8.36 us  [the longest x12 7.09 us: choose(): near = held if near is None else jnp.where(wanted == bit, held, near)]
    all_to_all x1 -> x0, starting transfers between devices: 7.42 us -> none  [gather_panels(): lax.all_to_all(pieces, 'col', split_axis=1, concat_axis=0, tiled=True)]
    reshape x0 -> x7, local copies, waits for them, and re-layouts: none -> 6.23 us  [the longest x4 6.2 us: spread_panels(): parts = [lax.dynamic_slice(blocks, (0, mine ^ bit, piece, 0, 0), (stored,...]
    ppermute x6, starting transfers between devices: 4.12 us -> 8.62 us  [tile_sum(): lax.ppermute(value, 'tile', [(i, i ^ step) for i in range(count)])]
  transfers between devices with their start and end apart: 36 -> 62, of which waited for: 19 -> 47; matrix products, arithmetic and copies ran while one was open for 11% -> 6% of each run, Pallas kernels for 0% -> 0%
where the time goes in v2:
time: 435 us; the launch traced here: 429 us
  waiting for transfers between devices  289 us (66%)
  starting transfers between devices  82.3 us (19%)
  other arithmetic  23.8 us (5%)
  matrix products  16.3 us (4%)
  local copies, waits for them, and re-layouts  15.1 us (3%)
    ppermute x48, waiting for transfers between devices, exchange(): return lax.ppermute(value, 'col', [(i, i ^ bit) for i in range(count)])  275 us
    ppermute x48, starting transfers between devices, exchange(): return lax.ppermute(value, 'col', [(i, i ^ bit) for i in range(count)])  60.9 us
    ppermute x6, waiting for transfers between devices, tile_sum(): lax.ppermute(value, 'tile', [(i, i ^ step) for i in range(count)])  13.1 us
    ppermute x8, starting transfers between devices, shifted(): return lax.ppermute(value, axis, pairs)  12.8 us
    dot_general x3, matrix products, per_device(): lax.dot_general(operator_panel, change, (((0,), (0,)), ((), ())), precisi...  10.7 us
  transfers between devices with their start and end apart: 62, of which 47 were waited for; matrix products, arithmetic and copies ran while one was open for 6% of the time, Pallas kernels for 0%

profile of v2, /device:TPU:0, one launch (start us, length us, event | category | flops | bytes accessed | tf_op | source)
XLA Modules:
  0.0 428.7 jit_solution(12866555924158594873)
XLA Ops:
  0.7 2.3 dynamic-slice_bitcast_fusion.12
  2.9 2.1 dynamic-slice_bitcast_fusion.8
  6.9 3.0 collective-permute-start.22
  11.4 1.9 collective-permute-start.16
  21.8 1.9 collective-permute-start.10
  24.5 2.0 collective-permute-start.11
  26.7 2.5 collective-permute-done.16
  29.2 3.7 collective-permute-start.12
  35.7 2.0 collective-permute-start.5
  37.8 2.4 collective-permute-done.10
  40.3 3.7 collective-permute-start.6
  50.0 2.9 collective-permute-start.57
  53.1 2.6 collective-permute-start.54
  55.6 4.7 %collective-permute-done.6 = f32[1,16,4096]{2,1,0:T(8,128)S(1)} collective-permute-done((f32[1,16,4096]{2,1,0:T(8,128)}, f32[1,16,4096]{2,1,0:T(8,128)S(1)}, u32[]{:S(2)}, u32[]{:S(2)}) %collective-permute-start.6) | collective-permute-done | bytes 262176 | tf_op jit(solution)/shard_map/ppermute | solution.py:64
  73.6 2.0 collective-permute-start.48
  76.8 2.2 collective-permute-start.41
  81.9 17.2 %collective-permute-done.54 = f32[16,4096]{1,0:T(8,128)S(1)} collective-permute-done((f32[16,4096]{1,0:T(8,128)S(1)}, f32[16,4096]{1,0:T(8,128)S(1)}, u32[]{:S(2)}, u32[]{:S(2)}) %collective-permute-start.54) | collective-permute-done | bytes 262176 | tf_op jit(solution)/shard_map/ppermute | solution.py:64
  99.2 11.2 %collective-permute-done.51 = f32[16,4096]{1,0:T(8,128)S(1)} collective-permute-done((f32[16,4096]{1,0:T(8,128)S(1)}, f32[16,4096]{1,0:T(8,128)S(1)}, u32[]{:S(2)}, u32[]{:S(2)}) %collective-permute-start.51) | collective-permute-done | bytes 262176 | tf_op jit(solution)/shard_map/ppermute | solution.py:64
  110.4 11.2 %collective-permute-done.48 = f32[16,4096]{1,0:T(8,128)S(1)} collective-permute-done((f32[16,4096]{1,0:T(8,128)S(1)}, f32[16,4096]{1,0:T(8,128)S(1)}, u32[]{:S(2)}, u32[]{:S(2)}) %collective-permute-start.48) | collective-permute-done | bytes 262176 | tf_op jit(solution)/shard_map/ppermute | solution.py:64
  121.7 11.2 %collective-permute-done.41 = f32[16,4096]{1,0:T(8,128)S(1)} collective-permute-done((f32[16,4096]{1,0:T(8,128)S(1)}, f32[16,4096]{1,0:T(8,128)S(1)}, u32[]{:S(2)}, u32[]{:S(2)}) %collective-permute-start.41) | collective-permute-done | bytes 262176 | tf_op jit(solution)/shard_map/ppermute | solution.py:64
  132.9 11.2 %collective-permute-done.38 = f32[16,4096]{1,0:T(8,128)S(1)} collective-permute-done((f32[16,4096]{1,0:T(8,128)S(1)}, f32[16,4096]{1,0:T(8,128)S(1)}, u32[]{:S(2)}, u32[]{:S(2)}) %collective-permute-start.38) | collective-permute-done | bytes 262176 | tf_op jit(solution)/shard_map/ppermute | solution.py:64
  144.1 11.2 %collective-permute-done.35 = f32[16,4096]{1,0:T(8,128)S(1)} collective-permute-done((f32[16,4096]{1,0:T(8,128)S(1)}, f32[16,4096]{1,0:T(8,128)S(1)}, u32[]{:S(2)}, u32[]{:S(2)}) %collective-permute-start.35) | collective-permute-done | bytes 262176 | tf_op jit(solution)/shard_map/ppermute | solution.py:64
  155.4 11.2 %collective-permute-done.32 = f32[16,4096]{1,0:T(8,128)S(1)} collective-permute-done((f32[16,4096]{1,0:T(8,128)S(1)}, f32[16,4096]{1,0:T(8,128)S(1)}, u32[]{:S(2)}, u32[]{:S(2)}) %collective-permute-start.32) | collective-permute-done | bytes 262176 | tf_op jit(solution)/shard_map/ppermute | solution.py:64
  168.0 4.3 %collective-permute-done.25 = f32[16,4096]{1,0:T(8,128)S(1)} collective-permute-done((f32[16,4096]{1,0:T(8,128)S(1)}, f32[16,4096]{1,0:T(8,128)S(1)}, u32[]{:S(2)}, u32[]{:S(2)}) %collective-permute-start.25) | collective-permute-done | bytes 262176 | tf_op jit(solution)/shard_map/ppermute | solution.py:64
  173.6 4.3 collective-permute-done.19
  179.3 4.3 collective-permute-done.13
  184.9 4.3 collective-permute-done.7
  190.5 4.5 %collective-permute-done.58 = f32[16,4096]{1,0:T(8,128)S(1)} collective-permute-done((f32[16,4096]{1,0:T(8,128)S(1)}, f32[16,4096]{1,0:T(8,128)S(1)}, u32[]{:S(2)}, u32[]{:S(2)}) %collective-permute-start.58) | collective-permute-done | bytes 262176 | tf_op jit(solution)/shard_map/ppermute | solution.py:64
  195.1 5.6 %collective-permute-done.55 = f32[16,4096]{1,0:T(8,128)S(1)} collective-permute-done((f32[16,4096]{1,0:T(8,128)S(1)}, f32[16,4096]{1,0:T(8,128)S(1)}, u32[]{:S(2)}, u32[]{:S(2)}) %collective-permute-start.55) | collective-permute-done | bytes 262176 | tf_op jit(solution)/shard_map/ppermute | solution.py:64
  200.7 5.6 %collective-permute-done.52 = f32[16,4096]{1,0:T(8,128)S(1)} collective-permute-done((f32[16,4096]{1,0:T(8,128)S(1)}, f32[16,4096]{1,0:T(8,128)S(1)}, u32[]{:S(2)}, u32[]{:S(2)}) %collective-permute-start.52) | collective-permute-done | bytes 262176 | tf_op jit(solution)/shard_map/ppermute | solution.py:64
  206.3 5.6 %collective-permute-done.49 = f32[16,4096]{1,0:T(8,128)S(1)} collective-permute-done((f32[16,4096]{1,0:T(8,128)S(1)}, f32[16,4096]{1,0:T(8,128)S(1)}, u32[]{:S(2)}, u32[]{:S(2)}) %collective-permute-start.49) | collective-permute-done | bytes 262176 | tf_op jit(solution)/shard_map/ppermute | solution.py:64
  211.9 5.6 %collective-permute-done.42 = f32[16,4096]{1,0:T(8,128)S(1)} collective-permute-done((f32[16,4096]{1,0:T(8,128)S(1)}, f32[16,4096]{1,0:T(8,128)S(1)}, u32[]{:S(2)}, u32[]{:S(2)}) %collective-permute-start.42) | collective-permute-done | bytes 262176 | tf_op jit(solution)/shard_map/ppermute | solution.py:64
  217.5 5.6 %collective-permute-done.39 = f32[16,4096]{1,0:T(8,128)S(1)} collective-permute-done((f32[16,4096]{1,0:T(8,128)S(1)}, f32[16,4096]{1,0:T(8,128)S(1)}, u32[]{:S(2)}, u32[]{:S(2)}) %collective-permute-start.39) | collective-permute-done | bytes 262176 | tf_op jit(solution)/shard_map/ppermute | solution.py:64
  223.1 5.6 %collective-permute-done.36 = f32[16,4096]{1,0:T(8,128)S(1)} collective-permute-done((f32[16,4096]{1,0:T(8,128)S(1)}, f32[16,4096]{1,0:T(8,128)S(1)}, u32[]{:S(2)}, u32[]{:S(2)}) %collective-permute-start.36) | collective-permute-done | bytes 262176 | tf_op jit(solution)/shard_map/ppermute | solution.py:64
  228.8 5.6 %collective-permute-done.33 = f32[16,4096]{1,0:T(8,128)S(1)} collective-permute-done((f32[16,4096]{1,0:T(8,128)S(1)}, f32[16,4096]{1,0:T(8,128)S(1)}, u32[]{:S(2)}, u32[]{:S(2)}) %collective-permute-start.33) | collective-permute-done | bytes 262176 | tf_op jit(solution)/shard_map/ppermute | solution.py:64
  236.3 3.7 collective-permute-done.26
  240.0 1.9 collective-permute-start.56
  241.9 3.7 collective-permute-done.20
  247.5 3.7 collective-permute-done.14
  253.1 3.7 collective-permute-done.8
  262.3 9.3 %collective-permute-done.53 = f32[32,4096]{1,0:T(8,128)S(1)} collective-permute-done((f32[32,4096]{1,0:T(8,128)S(1)}, f32[32,4096]{1,0:T(8,128)S(1)}, u32[]{:S(2)}, u32[]{:S(2)}) %collective-permute-start.53) | collective-permute-done | bytes 524320 | tf_op jit(solution)/shard_map/ppermute | solution.py:64
  271.6 1.9 collective-permute-start.34
  273.5 9.3 %collective-permute-done.50 = f32[32,4096]{1,0:T(8,128)S(1)} collective-permute-done((f32[32,4096]{1,0:T(8,128)S(1)}, f32[32,4096]{1,0:T(8,128)S(1)}, u32[]{:S(2)}, u32[]{:S(2)}) %collective-permute-start.50) | collective-permute-done | bytes 524320 | tf_op jit(solution)/shard_map/ppermute | solution.py:64
  282.8 1.9 collective-permute-start.27
  284.7 9.4 %collective-permute-done.43 = f32[32,4096]{1,0:T(8,128)S(1)} collective-permute-done((f32[32,4096]{1,0:T(8,128)S(1)}, f32[32,4096]{1,0:T(8,128)S(1)}, u32[]{:S(2)}, u32[]{:S(2)}) %collective-permute-start.43) | collective-permute-done | bytes 524320 | tf_op jit(solution)/shard_map/ppermute | solution.py:64
  294.1 1.9 collective-permute-start.21
  296.0 9.4 %collective-permute-done.40 = f32[32,4096]{1,0:T(8,128)S(1)} collective-permute-done((f32[32,4096]{1,0:T(8,128)S(1)}, f32[32,4096]{1,0:T(8,128)S(1)}, u32[]{:S(2)}, u32[]{:S(2)}) %collective-permute-start.40) | collective-permute-done | bytes 524320 | tf_op jit(solution)/shard_map/ppermute | solution.py:64
  307.2 9.4 %collective-permute-done.37 = f32[32,4096]{1,0:T(8,128)S(1)} collective-permute-done((f32[32,4096]{1,0:T(8,128)S(1)}, f32[32,4096]{1,0:T(8,128)S(1)}, u32[]{:S(2)}, u32[]{:S(2)}) %collective-permute-start.37) | collective-permute-done | bytes 524320 | tf_op jit(solution)/shard_map/ppermute | solution.py:64
  318.4 9.3 %collective-permute-done.34 = f32[32,4096]{1,0:T(8,128)S(1)} collective-permute-done((f32[32,4096]{1,0:T(8,128)S(1)}, f32[32,4096]{1,0:T(8,128)S(1)}, u32[]{:S(2)}, u32[]{:S(2)}) %collective-permute-start.34) | collective-permute-done | bytes 524320 | tf_op jit(solution)/shard_map/ppermute | solution.py:64
  327.8 11.2 %collective-permute-done.27 = f32[32,4096]{1,0:T(8,128)S(1)} collective-permute-done((f32[32,4096]{1,0:T(8,128)S(1)}, f32[32,4096]{1,0:T(8,128)S(1)}, u32[]{:S(2)}, u32[]{:S(2)}) %collective-permute-start.27) | collective-permute-done | bytes 524320 | tf_op jit(solution)/shard_map/ppermute | solution.py:64
  339.0 11.2 %collective-permute-done.21 = f32[32,4096]{1,0:T(8,128)S(1)} collective-permute-done((f32[32,4096]{1,0:T(8,128)S(1)}, f32[32,4096]{1,0:T(8,128)S(1)}, u32[]{:S(2)}, u32[]{:S(2)}) %collective-permute-start.21) | collective-permute-done | bytes 524320 | tf_op jit(solution)/shard_map/ppermute | solution.py:64
  350.3 11.2 %collective-permute-done.15 = f32[32,4096]{1,0:T(8,128)S(1)} collective-permute-done((f32[32,4096]{1,0:T(8,128)S(1)}, f32[32,4096]{1,0:T(8,128)S(1)}, u32[]{:S(2)}, u32[]{:S(2)}) %collective-permute-start.15) | collective-permute-done | bytes 524320 | tf_op jit(solution)/shard_map/ppermute | solution.py:64
  361.5 10.4 %collective-permute-done.9 = f32[32,4096]{1,0:T(8,128)S(1)} collective-permute-done((f32[32,4096]{1,0:T(8,128)S(1)}, f32[32,4096]{1,0:T(8,128)S(1)}, u32[]{:S(2)}, u32[]{:S(2)}) %collective-permute-start.9) | collective-permute-done | bytes 524320 | tf_op jit(solution)/shard_map/ppermute | solution.py:64
  376.3 1.9 collective-permute-start.29
  378.2 3.8 collective-permute-done.29
  382.0 3.7 fusion.70
  388.5 2.4 collective-permute-start.30
  392.4 3.7 collective-permute-start.45
  398.4 4.2 collective-permute-done.45
  402.7 3.5 fusion.61
  409.6 1.9 collective-permute-start.46
  413.1 2.3 collective-permute-start.61
  417.8 4.5 %collective-permute-done.61 = f32[256,128]{1,0:T(8,128)S(1)} collective-permute-done((f32[256,128]{1,0:T(8,128)S(1)}, f32[256,128]{1,0:T(8,128)S(1)}, u32[]{:S(2)}, u32[]{:S(2)}) %collective-permute-start.61) | collective-permute-done | bytes 131104 | tf_op jit(solution)/shard_map/ppermute | solution.py:57
  422.3 3.5 fusion.59
  (246 shorter events, 82.0 us)
Async XLA Ops:
  5.9 11.1 %copy-start = (f32[4096,128]{1,0:T(8,128)S(1)}, f32[4096,128]{1,0:T(8,128)}, u32[]{:S(2)}) copy-start(f32[4096,128]{1,0:T(8,128)} %param.5) | copy-start | bytes 6291460
  6.9 11.0 %copy-start.6 = (f32[3]{0:T(128)S(1)}, f32[3]{0:T(128)}, u32[]{:S(2)}) copy-start(f32[3]{0:T(128)} %param.9) | copy-start | bytes 40
  6.9 14.8 %collective-permute-start.22 = (f32[1,16,4096]{2,1,0:T(8,128)}, f32[1,16,4096]{2,1,0:T(8,128)S(1)}, u32[]{:S(2)}, u32[]{:S(2)}) collective-permute-start(f32[1,16,4096]{2,1,0:T(8,128)} %get-tuple-element.178), channel_id=1, source_target_pairs={{0,4},{4,0},{8,12},{12,8},{16,20},{20,16},{24,28},{28,24},{1,5},{5... | collective-permute-start | bytes 786440 | tf_op jit(solution)/shard_map/ppermute | solution.py:64
  9.8 12.0 %collective-permute-start.23 = (f32[1,16,4096]{2,1,0:T(8,128)}, f32[1,16,4096]{2,1,0:T(8,128)}, u32[]{:S(2)}, u32[]{:S(2)}) collective-permute-start(f32[1,16,4096]{2,1,0:T(8,128)} %get-tuple-element.179), channel_id=1, source_target_pairs={{0,8},{4,12},{8,0},{12,4},{16,24},{20,28},{24,16},{28,20},{1,9},{5... | collective-permute-start | bytes 786440 | tf_op jit(solution)/shard_map/ppermute | solution.py:64
  11.4 13.1 %collective-permute-start.24 = (f32[1,16,4096]{2,1,0:T(8,128)}, f32[1,16,4096]{2,1,0:T(8,128)}, u32[]{:S(2)}, u32[]{:S(2)}) collective-permute-start(f32[1,16,4096]{2,1,0:T(8,128)} %get-tuple-element.180), channel_id=1, source_target_pairs={{0,12},{4,8},{8,4},{12,0},{16,28},{20,24},{24,20},{28,16},{1,13},{... | collective-permute-start | bytes 786440 | tf_op jit(solution)/shard_map/ppermute | solution.py:64
  11.4 17.8 %collective-permute-start.16 = (f32[1,16,4096]{2,1,0:T(8,128)}, f32[1,16,4096]{2,1,0:T(8,128)}, u32[]{:S(2)}, u32[]{:S(2)}) collective-permute-start(f32[1,16,4096]{2,1,0:T(8,128)} %get-tuple-element.166), channel_id=1, source_target_pairs={{0,4},{4,0},{8,12},{12,8},{16,20},{20,16},{24,28},{28,24},{1,5},{5... | collective-permute-start | bytes 786440 | tf_op jit(solution)/shard_map/ppermute | solution.py:64
  13.3 20.7 %collective-permute-start.17 = (f32[1,16,4096]{2,1,0:T(8,128)}, f32[1,16,4096]{2,1,0:T(8,128)}, u32[]{:S(2)}, u32[]{:S(2)}) collective-permute-start(f32[1,16,4096]{2,1,0:T(8,128)} %get-tuple-element.167), channel_id=1, source_target_pairs={{0,8},{4,12},{8,0},{12,4},{16,24},{20,28},{24,16},{28,20},{1,9},{5... | collective-permute-start | bytes 786440 | tf_op jit(solution)/shard_map/ppermute | solution.py:64
  21.7 14.0 %collective-permute-start.18 = (f32[1,16,4096]{2,1,0:T(8,128)}, f32[1,16,4096]{2,1,0:T(8,128)S(1)}, u32[]{:S(2)}, u32[]{:S(2)}) collective-permute-start(f32[1,16,4096]{2,1,0:T(8,128)} %get-tuple-element.168), channel_id=1, source_target_pairs={{0,12},{4,8},{8,4},{12,0},{16,28},{20,24},{24,20},{28,16},{1,13},{... | collective-permute-start | bytes 786440 | tf_op jit(solution)/shard_map/ppermute | solution.py:64
  21.8 18.5 %collective-permute-start.10 = (f32[1,16,4096]{2,1,0:T(8,128)}, f32[1,16,4096]{2,1,0:T(8,128)S(1)}, u32[]{:S(2)}, u32[]{:S(2)}) collective-permute-start(f32[1,16,4096]{2,1,0:T(8,128)} %get-tuple-element.154), channel_id=1, source_target_pairs={{0,4},{4,0},{8,12},{12,8},{16,20},{20,16},{24,28},{28,24},{1,5},{5... | collective-permute-start | bytes 786440 | tf_op jit(solution)/shard_map/ppermute | solution.py:64
  24.5 19.5 %collective-permute-start.11 = (f32[1,16,4096]{2,1,0:T(8,128)}, f32[1,16,4096]{2,1,0:T(8,128)S(1)}, u32[]{:S(2)}, u32[]{:S(2)}) collective-permute-start(f32[1,16,4096]{2,1,0:T(8,128)} %get-tuple-element.155), channel_id=1, source_target_pairs={{0,8},{4,12},{8,0},{12,4},{16,24},{20,28},{24,16},{28,20},{1,9},{5... | collective-permute-start | bytes 786440 | tf_op jit(solution)/shard_map/ppermute | solution.py:64
  29.2 17.8 %collective-permute-start.12 = (f32[1,16,4096]{2,1,0:T(8,128)}, f32[1,16,4096]{2,1,0:T(8,128)S(1)}, u32[]{:S(2)}, u32[]{:S(2)}) collective-permute-start(f32[1,16,4096]{2,1,0:T(8,128)} %get-tuple-element.156), channel_id=1, source_target_pairs={{0,12},{4,8},{8,4},{12,0},{16,28},{20,24},{24,20},{28,16},{1,13},{... | collective-permute-start | bytes 786440 | tf_op jit(solution)/shard_map/ppermute | solution.py:64
  34.0 16.1 %collective-permute-start.4 = (f32[1,16,4096]{2,1,0:T(8,128)}, f32[1,16,4096]{2,1,0:T(8,128)S(1)}, u32[]{:S(2)}, u32[]{:S(2)}) collective-permute-start(f32[1,16,4096]{2,1,0:T(8,128)} %get-tuple-element.142), channel_id=1, source_target_pairs={{0,4},{4,0},{8,12},{12,8},{16,20},{20,16},{24,28},{28,24},{1,5},{5... | collective-permute-start | bytes 786440 | tf_op jit(solution)/shard_map/ppermute | solution.py:64
  35.7 17.4 %collective-permute-start.5 = (f32[1,16,4096]{2,1,0:T(8,128)}, f32[1,16,4096]{2,1,0:T(8,128)S(1)}, u32[]{:S(2)}, u32[]{:S(2)}) collective-permute-start(f32[1,16,4096]{2,1,0:T(8,128)} %get-tuple-element.143), channel_id=1, source_target_pairs={{0,8},{4,12},{8,0},{12,4},{16,24},{20,28},{24,16},{28,20},{1,9},{5... | collective-permute-start | bytes 786440 | tf_op jit(solution)/shard_map/ppermute | solution.py:64
  40.3 20.0 %collective-permute-start.6 = (f32[1,16,4096]{2,1,0:T(8,128)}, f32[1,16,4096]{2,1,0:T(8,128)S(1)}, u32[]{:S(2)}, u32[]{:S(2)}) collective-permute-start(f32[1,16,4096]{2,1,0:T(8,128)} %get-tuple-element.144), channel_id=1, source_target_pairs={{0,12},{4,8},{8,4},{12,0},{16,28},{20,24},{24,20},{28,16},{1,13},{... | collective-permute-start | bytes 786440 | tf_op jit(solution)/shard_map/ppermute | solution.py:64
  44.0 23.7 %collective-permute-start = (f32[1,512,128]{2,1,0:T(8,128)}, f32[1,512,128]{2,1,0:T(8,128)S(1)}, u32[]{:S(2)}, u32[]{:S(2)}) collective-permute-start(f32[1,512,128]{2,1,0:T(8,128)} %get-tuple-element.352), channel_id=1, source_target_pairs={{0,1},{1,2},{2,3},{4,5},{5,6},{6,7},{8,9},{9,10},{10,11},{12,13},{... | collective-permute-start | bytes 786440 | tf_op jit(solution)/shard_map/ppermute | solution.py:21
  47.0 21.0 %collective-permute-start.1 = (f32[1,512,128]{2,1,0:T(8,128)}, f32[1,512,128]{2,1,0:T(8,128)S(1)}, u32[]{:S(2)}, u32[]{:S(2)}) collective-permute-start(f32[1,512,128]{2,1,0:T(8,128)} %get-tuple-element.351), channel_id=1, source_target_pairs={{1,0},{2,1},{3,2},{5,4},{6,5},{7,6},{9,8},{10,9},{11,10},{13,12},{... | collective-permute-start | bytes 786440 | tf_op jit(solution)/shard_map/ppermute | solution.py:21
  50.0 31.0 %collective-permute-start.57 = (f32[16,4096]{1,0:T(8,128)S(1)}, f32[16,4096]{1,0:T(8,128)S(1)}, u32[]{:S(2)}, u32[]{:S(2)}) collective-permute-start(f32[16,4096]{1,0:T(8,128)S(1)} %fusion.36), channel_id=1, source_target_pairs={{0,16},{4,20},{8,24},{12,28},{16,0},{20,4},{24,8},{28,12},{1,17},{... | collective-permute-start | bytes 786440 | tf_op jit(solution)/shard_map/ppermute | solution.py:64
  53.1 46.1 %collective-permute-start.54 = (f32[16,4096]{1,0:T(8,128)S(1)}, f32[16,4096]{1,0:T(8,128)S(1)}, u32[]{:S(2)}, u32[]{:S(2)}) collective-permute-start(f32[16,4096]{1,0:T(8,128)S(1)} %fusion.38), channel_id=1, source_target_pairs={{0,16},{4,20},{8,24},{12,28},{16,0},{20,4},{24,8},{28,12},{1,17},{... | collective-permute-start | bytes 786440 | tf_op jit(solution)/shard_map/ppermute | solution.py:64
  60.3 50.1 %collective-permute-start.51 = (f32[16,4096]{1,0:T(8,128)S(1)}, f32[16,4096]{1,0:T(8,128)S(1)}, u32[]{:S(2)}, u32[]{:S(2)}) collective-permute-start(f32[16,4096]{1,0:T(8,128)S(1)} %fusion.40), channel_id=1, source_target_pairs={{0,16},{4,20},{8,24},{12,28},{16,0},{20,4},{24,8},{28,12},{1,17},{... | collective-permute-start | bytes 786440 | tf_op jit(solution)/shard_map/ppermute | solution.py:64
  70.2 3.4 collective-permute-start.2
  71.7 5.1 %collective-permute-start.3 = (f32[1,512,128]{2,1,0:T(8,128)S(1)}, f32[1,512,128]{2,1,0:T(8,128)S(1)}, u32[]{:S(2)}, u32[]{:S(2)}) collective-permute-start(f32[1,512,128]{2,1,0:T(8,128)S(1)} %get-tuple-element.349), channel_id=1, source_target_pairs={{1,0},{2,1},{3,2},{5,4},{6,5},{7,6},{9,8},{10,9},{11,10},{13,12},{... | collective-permute-start | bytes 786440 | tf_op jit(solution)/shard_map/ppermute | solution.py:21
  73.6 48.0 %collective-permute-start.48 = (f32[16,4096]{1,0:T(8,128)S(1)}, f32[16,4096]{1,0:T(8,128)S(1)}, u32[]{:S(2)}, u32[]{:S(2)}) collective-permute-start(f32[16,4096]{1,0:T(8,128)S(1)} %fusion.42), channel_id=1, source_target_pairs={{0,16},{4,20},{8,24},{12,28},{16,0},{20,4},{24,8},{28,12},{1,17},{... | collective-permute-start | bytes 786440 | tf_op jit(solution)/shard_map/ppermute | solution.py:64
  76.8 56.0 %collective-permute-start.41 = (f32[16,4096]{1,0:T(8,128)S(1)}, f32[16,4096]{1,0:T(8,128)S(1)}, u32[]{:S(2)}, u32[]{:S(2)}) collective-permute-start(f32[16,4096]{1,0:T(8,128)S(1)} %fusion.44), channel_id=1, source_target_pairs={{0,16},{4,20},{8,24},{12,28},{16,0},{20,4},{24,8},{28,12},{1,17},{... | collective-permute-start | bytes 786440 | tf_op jit(solution)/shard_map/ppermute | solution.py:64
  81.1 63.0 %collective-permute-start.38 = (f32[16,4096]{1,0:T(8,128)S(1)}, f32[16,4096]{1,0:T(8,128)S(1)}, u32[]{:S(2)}, u32[]{:S(2)}) collective-permute-start(f32[16,4096]{1,0:T(8,128)S(1)} %fusion.46), channel_id=1, source_target_pairs={{0,16},{4,20},{8,24},{12,28},{16,0},{20,4},{24,8},{28,12},{1,17},{... | collective-permute-start | bytes 786440 | tf_op jit(solution)/shard_map/ppermute | solution.py:64
  99.2 56.2 %collective-permute-start.35 = (f32[16,4096]{1,0:T(8,128)S(1)}, f32[16,4096]{1,0:T(8,128)S(1)}, u32[]{:S(2)}, u32[]{:S(2)}) collective-permute-start(f32[16,4096]{1,0:T(8,128)S(1)} %fusion.48), channel_id=1, source_target_pairs={{0,16},{4,20},{8,24},{12,28},{16,0},{20,4},{24,8},{28,12},{1,17},{... | collective-permute-start | bytes 786440 | tf_op jit(solution)/shard_map/ppermute | solution.py:64
  110.4 56.2 %collective-permute-start.32 = (f32[16,4096]{1,0:T(8,128)S(1)}, f32[16,4096]{1,0:T(8,128)S(1)}, u32[]{:S(2)}, u32[]{:S(2)}) collective-permute-start(f32[16,4096]{1,0:T(8,128)S(1)} %fusion.50), channel_id=1, source_target_pairs={{0,16},{4,20},{8,24},{12,28},{16,0},{20,4},{24,8},{28,12},{1,17},{... | collective-permute-start | bytes 786440 | tf_op jit(solution)/shard_map/ppermute | solution.py:64
  121.6 50.7 %collective-permute-start.25 = (f32[16,4096]{1,0:T(8,128)S(1)}, f32[16,4096]{1,0:T(8,128)S(1)}, u32[]{:S(2)}, u32[]{:S(2)}) collective-permute-start(f32[16,4096]{1,0:T(8,128)S(1)} %fusion.52), channel_id=1, source_target_pairs={{0,16},{4,20},{8,24},{12,28},{16,0},{20,4},{24,8},{28,12},{1,17},{... | collective-permute-start | bytes 786440 | tf_op jit(solution)/shard_map/ppermute | solution.py:64
  132.9 45.0 %collective-permute-start.19 = (f32[16,4096]{1,0:T(8,128)S(1)}, f32[16,4096]{1,0:T(8,128)S(1)}, u32[]{:S(2)}, u32[]{:S(2)}) collective-permute-start(f32[16,4096]{1,0:T(8,128)S(1)} %fusion.54), channel_id=1, source_target_pairs={{0,16},{4,20},{8,24},{12,28},{16,0},{20,4},{24,8},{28,12},{1,17},{... | collective-permute-start | bytes 786440 | tf_op jit(solution)/shard_map/ppermute | solution.py:64
  144.1 39.4 %collective-permute-start.13 = (f32[16,4096]{1,0:T(8,128)S(1)}, f32[16,4096]{1,0:T(8,128)S(1)}, u32[]{:S(2)}, u32[]{:S(2)}) collective-permute-start(f32[16,4096]{1,0:T(8,128)S(1)} %fusion.56), channel_id=1, source_target_pairs={{0,16},{4,20},{8,24},{12,28},{16,0},{20,4},{24,8},{28,12},{1,17},{... | collective-permute-start | bytes 786440 | tf_op jit(solution)/shard_map/ppermute | solution.py:64
  155.3 33.8 %collective-permute-start.7 = (f32[16,4096]{1,0:T(8,128)S(1)}, f32[16,4096]{1,0:T(8,128)S(1)}, u32[]{:S(2)}, u32[]{:S(2)}) collective-permute-start(f32[16,4096]{1,0:T(8,128)S(1)} %fusion.58), channel_id=1, source_target_pairs={{0,16},{4,20},{8,24},{12,28},{16,0},{20,4},{24,8},{28,12},{1,17},{... | collective-permute-start | bytes 786440 | tf_op jit(solution)/shard_map/ppermute | solution.py:64
  166.6 28.4 %collective-permute-start.58 = (f32[16,4096]{1,0:T(8,128)S(1)}, f32[16,4096]{1,0:T(8,128)S(1)}, u32[]{:S(2)}, u32[]{:S(2)}) collective-permute-start(f32[16,4096]{1,0:T(8,128)S(1)} %broadcast_select_fusion), channel_id=1, source_target_pairs={{0,8},{4,12},{8,0},{12,4},{16,24},{20,28},{24,16},{28,20},{1,9},{5... | collective-permute-start | bytes 786440 | tf_op jit(solution)/shard_map/ppermute | solution.py:64
  172.3 28.3 %collective-permute-start.55 = (f32[16,4096]{1,0:T(8,128)S(1)}, f32[16,4096]{1,0:T(8,128)S(1)}, u32[]{:S(2)}, u32[]{:S(2)}) collective-permute-start(f32[16,4096]{1,0:T(8,128)S(1)} %broadcast_select_fusion.1), channel_id=1, source_target_pairs={{0,8},{4,12},{8,0},{12,4},{16,24},{20,28},{24,16},{28,20},{1,9},{5... | collective-permute-start | bytes 786440 | tf_op jit(solution)/shard_map/ppermute | solution.py:64
  177.9 28.3 %collective-permute-start.52 = (f32[16,4096]{1,0:T(8,128)S(1)}, f32[16,4096]{1,0:T(8,128)S(1)}, u32[]{:S(2)}, u32[]{:S(2)}) collective-permute-start(f32[16,4096]{1,0:T(8,128)S(1)} %broadcast_select_fusion.2), channel_id=1, source_target_pairs={{0,8},{4,12},{8,0},{12,4},{16,24},{20,28},{24,16},{28,20},{1,9},{5... | collective-permute-start | bytes 786440 | tf_op jit(solution)/shard_map/ppermute | solution.py:64
  183.5 28.3 %collective-permute-start.49 = (f32[16,4096]{1,0:T(8,128)S(1)}, f32[16,4096]{1,0:T(8,128)S(1)}, u32[]{:S(2)}, u32[]{:S(2)}) collective-permute-start(f32[16,4096]{1,0:T(8,128)S(1)} %broadcast_select_fusion.3), channel_id=1, source_target_pairs={{0,8},{4,12},{8,0},{12,4},{16,24},{20,28},{24,16},{28,20},{1,9},{5... | collective-permute-start | bytes 786440 | tf_op jit(solution)/shard_map/ppermute | solution.py:64
  189.1 28.3 %collective-permute-start.42 = (f32[16,4096]{1,0:T(8,128)S(1)}, f32[16,4096]{1,0:T(8,128)S(1)}, u32[]{:S(2)}, u32[]{:S(2)}) collective-permute-start(f32[16,4096]{1,0:T(8,128)S(1)} %broadcast_select_fusion.4), channel_id=1, source_target_pairs={{0,8},{4,12},{8,0},{12,4},{16,24},{20,28},{24,16},{28,20},{1,9},{5... | collective-permute-start | bytes 786440 | tf_op jit(solution)/shard_map/ppermute | solution.py:64
  195.0 28.1 %collective-permute-start.39 = (f32[16,4096]{1,0:T(8,128)S(1)}, f32[16,4096]{1,0:T(8,128)S(1)}, u32[]{:S(2)}, u32[]{:S(2)}) collective-permute-start(f32[16,4096]{1,0:T(8,128)S(1)} %broadcast_select_fusion.5), channel_id=1, source_target_pairs={{0,8},{4,12},{8,0},{12,4},{16,24},{20,28},{24,16},{28,20},{1,9},{5... | collective-permute-start | bytes 786440 | tf_op jit(solution)/shard_map/ppermute | solution.py:64
  200.6 28.1 %collective-permute-start.36 = (f32[16,4096]{1,0:T(8,128)S(1)}, f32[16,4096]{1,0:T(8,128)S(1)}, u32[]{:S(2)}, u32[]{:S(2)}) collective-permute-start(f32[16,4096]{1,0:T(8,128)S(1)} %broadcast_select_fusion.6), channel_id=1, source_target_pairs={{0,8},{4,12},{8,0},{12,4},{16,24},{20,28},{24,16},{28,20},{1,9},{5... | collective-permute-start | bytes 786440 | tf_op jit(solution)/shard_map/ppermute | solution.py:64
  206.3 28.1 %collective-permute-start.33 = (f32[16,4096]{1,0:T(8,128)S(1)}, f32[16,4096]{1,0:T(8,128)S(1)}, u32[]{:S(2)}, u32[]{:S(2)}) collective-permute-start(f32[16,4096]{1,0:T(8,128)S(1)} %broadcast_select_fusion.7), channel_id=1, source_target_pairs={{0,8},{4,12},{8,0},{12,4},{16,24},{20,28},{24,16},{28,20},{1,9},{5... | collective-permute-start | bytes 786440 | tf_op jit(solution)/shard_map/ppermute | solution.py:64
  211.9 28.1 %collective-permute-start.26 = (f32[16,4096]{1,0:T(8,128)S(1)}, f32[16,4096]{1,0:T(8,128)S(1)}, u32[]{:S(2)}, u32[]{:S(2)}) collective-permute-start(f32[16,4096]{1,0:T(8,128)S(1)} %broadcast_select_fusion.8), channel_id=1, source_target_pairs={{0,8},{4,12},{8,0},{12,4},{16,24},{20,28},{24,16},{28,20},{1,9},{5... | collective-permute-start | bytes 786440 | tf_op jit(solution)/shard_map/ppermute | solution.py:64
  217.5 28.1 %collective-permute-start.20 = (f32[16,4096]{1,0:T(8,128)S(1)}, f32[16,4096]{1,0:T(8,128)S(1)}, u32[]{:S(2)}, u32[]{:S(2)}) collective-permute-start(f32[16,4096]{1,0:T(8,128)S(1)} %broadcast_select_fusion.9), channel_id=1, source_target_pairs={{0,8},{4,12},{8,0},{12,4},{16,24},{20,28},{24,16},{28,20},{1,9},{5... | collective-permute-start | bytes 786440 | tf_op jit(solution)/shard_map/ppermute | solution.py:64
  223.1 28.1 %collective-permute-start.14 = (f32[16,4096]{1,0:T(8,128)S(1)}, f32[16,4096]{1,0:T(8,128)S(1)}, u32[]{:S(2)}, u32[]{:S(2)}) collective-permute-start(f32[16,4096]{1,0:T(8,128)S(1)} %broadcast_select_fusion.10), channel_id=1, source_target_pairs={{0,8},{4,12},{8,0},{12,4},{16,24},{20,28},{24,16},{28,20},{1,9},{5... | collective-permute-start | bytes 786440 | tf_op jit(solution)/shard_map/ppermute | solution.py:64
  228.7 28.1 %collective-permute-start.8 = (f32[16,4096]{1,0:T(8,128)S(1)}, f32[16,4096]{1,0:T(8,128)S(1)}, u32[]{:S(2)}, u32[]{:S(2)}) collective-permute-start(f32[16,4096]{1,0:T(8,128)S(1)} %broadcast_select_fusion.11), channel_id=1, source_target_pairs={{0,8},{4,12},{8,0},{12,4},{16,24},{20,28},{24,16},{28,20},{1,9},{5... | collective-permute-start | bytes 786440 | tf_op jit(solution)/shard_map/ppermute | solution.py:64
  234.3 24.3 %collective-permute-start.59 = (f32[32,4096]{1,0:T(8,128)S(1)}, f32[32,4096]{1,0:T(8,128)S(1)}, u32[]{:S(2)}, u32[]{:S(2)}) collective-permute-start(f32[32,4096]{1,0:T(8,128)S(1)} %pad_maximum_fusion.15), channel_id=1, source_target_pairs={{0,4},{4,0},{8,12},{12,8},{16,20},{20,16},{24,28},{28,24},{1,5},{5... | collective-permute-start | bytes 1572872 | tf_op jit(solution)/shard_map/ppermute | solution.py:64
  240.0 20.4 %collective-permute-start.56 = (f32[32,4096]{1,0:T(8,128)S(1)}, f32[32,4096]{1,0:T(8,128)S(1)}, u32[]{:S(2)}, u32[]{:S(2)}) collective-permute-start(f32[32,4096]{1,0:T(8,128)S(1)} %pad_maximum_fusion.14), channel_id=1, source_target_pairs={{0,4},{4,0},{8,12},{12,8},{16,20},{20,16},{24,28},{28,24},{1,5},{5... | collective-permute-start | bytes 1572872 | tf_op jit(solution)/shard_map/ppermute | solution.py:64
  245.6 26.0 %collective-permute-start.53 = (f32[32,4096]{1,0:T(8,128)S(1)}, f32[32,4096]{1,0:T(8,128)S(1)}, u32[]{:S(2)}, u32[]{:S(2)}) collective-permute-start(f32[32,4096]{1,0:T(8,128)S(1)} %pad_maximum_fusion.13), channel_id=1, source_target_pairs={{0,4},{4,0},{8,12},{12,8},{16,20},{20,16},{24,28},{28,24},{1,5},{5... | collective-permute-start | bytes 1572872 | tf_op jit(solution)/shard_map/ppermute | solution.py:64
  251.2 31.6 %collective-permute-start.50 = (f32[32,4096]{1,0:T(8,128)S(1)}, f32[32,4096]{1,0:T(8,128)S(1)}, u32[]{:S(2)}, u32[]{:S(2)}) collective-permute-start(f32[32,4096]{1,0:T(8,128)S(1)} %pad_maximum_fusion.12), channel_id=1, source_target_pairs={{0,4},{4,0},{8,12},{12,8},{16,20},{20,16},{24,28},{28,24},{1,5},{5... | collective-permute-start | bytes 1572872 | tf_op jit(solution)/shard_map/ppermute | solution.py:64
  256.8 37.3 %collective-permute-start.43 = (f32[32,4096]{1,0:T(8,128)S(1)}, f32[32,4096]{1,0:T(8,128)S(1)}, u32[]{:S(2)}, u32[]{:S(2)}) collective-permute-start(f32[32,4096]{1,0:T(8,128)S(1)} %pad_maximum_fusion.11), channel_id=1, source_target_pairs={{0,4},{4,0},{8,12},{12,8},{16,20},{20,16},{24,28},{28,24},{1,5},{5... | collective-permute-start | bytes 1572872 | tf_op jit(solution)/shard_map/ppermute | solution.py:64
  258.6 46.7 %collective-permute-start.40 = (f32[32,4096]{1,0:T(8,128)S(1)}, f32[32,4096]{1,0:T(8,128)S(1)}, u32[]{:S(2)}, u32[]{:S(2)}) collective-permute-start(f32[32,4096]{1,0:T(8,128)S(1)} %pad_maximum_fusion.10), channel_id=1, source_target_pairs={{0,4},{4,0},{8,12},{12,8},{16,20},{20,16},{24,28},{28,24},{1,5},{5... | collective-permute-start | bytes 1572872 | tf_op jit(solution)/shard_map/ppermute | solution.py:64
  260.4 56.2 %collective-permute-start.37 = (f32[32,4096]{1,0:T(8,128)S(1)}, f32[32,4096]{1,0:T(8,128)S(1)}, u32[]{:S(2)}, u32[]{:S(2)}) collective-permute-start(f32[32,4096]{1,0:T(8,128)S(1)} %pad_maximum_fusion.9), channel_id=1, source_target_pairs={{0,4},{4,0},{8,12},{12,8},{16,20},{20,16},{24,28},{28,24},{1,5},{5... | collective-permute-start | bytes 1572872 | tf_op jit(solution)/shard_map/ppermute | solution.py:64
  271.6 56.2 %collective-permute-start.34 = (f32[32,4096]{1,0:T(8,128)S(1)}, f32[32,4096]{1,0:T(8,128)S(1)}, u32[]{:S(2)}, u32[]{:S(2)}) collective-permute-start(f32[32,4096]{1,0:T(8,128)S(1)} %pad_maximum_fusion.8), channel_id=1, source_target_pairs={{0,4},{4,0},{8,12},{12,8},{16,20},{20,16},{24,28},{28,24},{1,5},{5... | collective-permute-start | bytes 1572872 | tf_op jit(solution)/shard_map/ppermute | solution.py:64
  282.8 56.2 %collective-permute-start.27 = (f32[32,4096]{1,0:T(8,128)S(1)}, f32[32,4096]{1,0:T(8,128)S(1)}, u32[]{:S(2)}, u32[]{:S(2)}) collective-permute-start(f32[32,4096]{1,0:T(8,128)S(1)} %pad_maximum_fusion.7), channel_id=1, source_target_pairs={{0,4},{4,0},{8,12},{12,8},{16,20},{20,16},{24,28},{28,24},{1,5},{5... | collective-permute-start | bytes 1572872 | tf_op jit(solution)/shard_map/ppermute | solution.py:64
  294.1 56.2 %collective-permute-start.21 = (f32[32,4096]{1,0:T(8,128)S(1)}, f32[32,4096]{1,0:T(8,128)S(1)}, u32[]{:S(2)}, u32[]{:S(2)}) collective-permute-start(f32[32,4096]{1,0:T(8,128)S(1)} %pad_maximum_fusion.6), channel_id=1, source_target_pairs={{0,4},{4,0},{8,12},{12,8},{16,20},{20,16},{24,28},{28,24},{1,5},{5... | collective-permute-start | bytes 1572872 | tf_op jit(solution)/shard_map/ppermute | solution.py:64
  305.3 56.2 %collective-permute-start.15 = (f32[32,4096]{1,0:T(8,128)S(1)}, f32[32,4096]{1,0:T(8,128)S(1)}, u32[]{:S(2)}, u32[]{:S(2)}) collective-permute-start(f32[32,4096]{1,0:T(8,128)S(1)} %pad_maximum_fusion.5), channel_id=1, source_target_pairs={{0,4},{4,0},{8,12},{12,8},{16,20},{20,16},{24,28},{28,24},{1,5},{5... | collective-permute-start | bytes 1572872 | tf_op jit(solution)/shard_map/ppermute | solution.py:64
  316.5 55.3 %collective-permute-start.9 = (f32[32,4096]{1,0:T(8,128)S(1)}, f32[32,4096]{1,0:T(8,128)S(1)}, u32[]{:S(2)}, u32[]{:S(2)}) collective-permute-start(f32[32,4096]{1,0:T(8,128)S(1)} %pad_maximum_fusion.4), channel_id=1, source_target_pairs={{0,4},{4,0},{8,12},{12,8},{16,20},{20,16},{24,28},{28,24},{1,5},{5... | collective-permute-start | bytes 1572872 | tf_op jit(solution)/shard_map/ppermute | solution.py:64
  374.8 1.4 collective-permute-start.28
  376.3 5.7 %collective-permute-start.29 = (f32[256,128]{1,0:T(8,128)S(1)}, f32[256,128]{1,0:T(8,128)S(1)}, u32[]{:S(2)}, u32[]{:S(2)}) collective-permute-start(f32[256,128]{1,0:T(8,128)S(1)} %add.136), channel_id=1, source_target_pairs={{0,2},{1,3},{2,0},{3,1},{4,6},{5,7},{6,4},{7,5},{8,10},{9,11},{10,... | collective-permute-start | bytes 393224 | tf_op jit(solution)/shard_map/ppermute | solution.py:57
  388.5 3.9 collective-permute-start.44
  388.5 7.5 %collective-permute-start.30 = (f32[1,512,128]{2,1,0:T(8,128)S(1)}, f32[1,512,128]{2,1,0:T(8,128)S(1)}, u32[]{:S(2)}, u32[]{:S(2)}) collective-permute-start(f32[1,512,128]{2,1,0:T(8,128)S(1)} %get-tuple-element.348), channel_id=1, source_target_pairs={{0,1},{1,2},{2,3},{4,5},{5,6},{6,7},{8,9},{9,10},{10,11},{12,13},{... | collective-permute-start | bytes 786440 | tf_op jit(solution)/shard_map/ppermute | solution.py:21
  390.9 5.4 %collective-permute-start.31 = (f32[1,512,128]{2,1,0:T(8,128)S(1)}, f32[1,512,128]{2,1,0:T(8,128)S(1)}, u32[]{:S(2)}, u32[]{:S(2)}) collective-permute-start(f32[1,512,128]{2,1,0:T(8,128)S(1)} %get-tuple-element.347), channel_id=1, source_target_pairs={{1,0},{2,1},{3,2},{5,4},{6,5},{7,6},{9,8},{10,9},{11,10},{13,12},{... | collective-permute-start | bytes 786440 | tf_op jit(solution)/shard_map/ppermute | solution.py:21
  392.4 10.3 %collective-permute-start.45 = (f32[256,128]{1,0:T(8,128)S(1)}, f32[256,128]{1,0:T(8,128)S(1)}, u32[]{:S(2)}, u32[]{:S(2)}) collective-permute-start(f32[256,128]{1,0:T(8,128)S(1)} %add.144), channel_id=1, source_target_pairs={{0,2},{1,3},{2,0},{3,1},{4,6},{5,7},{6,4},{7,5},{8,10},{9,11},{10,... | collective-permute-start | bytes 393224 | tf_op jit(solution)/shard_map/ppermute | solution.py:57
  409.0 4.1 collective-permute-start.60
  409.6 5.9 %collective-permute-start.46 = (f32[1,512,128]{2,1,0:T(8,128)S(1)}, f32[1,512,128]{2,1,0:T(8,128)S(1)}, u32[]{:S(2)}, u32[]{:S(2)}) collective-permute-start(f32[1,512,128]{2,1,0:T(8,128)S(1)} %get-tuple-element.346), channel_id=1, source_target_pairs={{0,1},{1,2},{2,3},{4,5},{5,6},{6,7},{8,9},{9,10},{10,11},{12,13},{... | collective-permute-start | bytes 786440 | tf_op jit(solution)/shard_map/ppermute | solution.py:21
  411.6 4.1 collective-permute-start.47
  413.1 9.1 %collective-permute-start.61 = (f32[256,128]{1,0:T(8,128)S(1)}, f32[256,128]{1,0:T(8,128)S(1)}, u32[]{:S(2)}, u32[]{:S(2)}) collective-permute-start(f32[256,128]{1,0:T(8,128)S(1)} %add.153), channel_id=1, source_target_pairs={{0,2},{1,3},{2,0},{3,1},{4,6},{5,7},{6,4},{7,5},{8,10},{9,11},{10,... | collective-permute-start | bytes 393224 | tf_op jit(solution)/shard_map/ppermute | solution.py:57
  (5 other events, 17.0 us)
